TPU v7x, 32 devices: a whole 2x2x4 slice. The times are simulated.
32 devices in a mesh: groups: 2 (over y), hosts: 4 (over z), mp: 4 (over x, core).
Axes of the slice: x: 2, y: 2, z: 4, core: 2. Of those that a mesh axis runs over, the one named last changes fastest.
Arguments:
- hidden: bfloat16 [256, 4096], P(('groups', 'hosts'), 'mp'), parts along dimension 0, may hold values from -6 to 6
- base_query_projection: bfloat16 [256, 4096], P(('groups', 'hosts'), 'mp'), parts along dimension 0, may hold values from -160 to 160
- base_key_projection: bfloat16 [256, 4096], P(('groups', 'hosts'), 'mp'), parts along dimension 0, may hold values from -6 to 6
- base_value_projection: bfloat16 [256, 4096], P(('groups', 'hosts'), 'mp'), parts along dimension 0, may hold values from -6 to 6
- adapter_input_factors: bfloat16 [8, 4096, 128], P(('groups', 'hosts'), 'mp'), parts along dimension 0, may hold values from -0.09375 to 0.09375
- adapter_output_factors: bfloat16 [8, 2, 64, 4096], P(('groups', 'hosts'), None, None, 'mp'), parts along dimension 0, may hold values from -0.75 to 0.75
- statement_prefix_cache: bfloat16 [32, 2, 128, 4096], P(('groups', 'hosts'), None, None, 'mp'), parts along dimension 0, may hold values from -6 to 6
- generated_token_cache: bfloat16 [256, 2, 8, 4096], P(('groups', 'hosts'), None, None, 'mp'), parts along dimension 0, may hold values from -6 to 6
- attempt_theorem_index: int32 [256], P(('groups', 'hosts')), parts along dimension 0, may hold values from 0 to 3, as said below
- host_live_count: int32 [8], P(('groups', 'hosts')), parts along dimension 0, may hold values from 8 to 32, as said below
- adapter_pool_row: int32 [8], P('groups'), parts along dimension 0, may hold values from 0 to 3, as said below
- prefix_pool_row: int32 [8, 4], P('groups'), parts along dimension 0, may hold values from 0 to 15, as said below
- prefix_block_count: int32 [8], P('groups'), parts along dimension 0, may hold values from 1 to 4
Outputs:
- attended: bfloat16 [256, 4096], P(('groups', 'hosts'), 'mp'), parts along dimension 0
- key_rows: bfloat16 [256, 4096], P(('groups', 'hosts'), 'mp'), parts along dimension 0
- value_rows: bfloat16 [256, 4096], P(('groups', 'hosts'), 'mp'), parts along dimension 0
There are 2 independent parts, one for each index of `groups`. A program takes and returns all parts, laid end to end along the dimension named above; each array names one. Nothing has to cross between parts.
Inputs may be any that keep to these rules, and one draw needn't show every extreme that they name: `attempt_theorem_index`: among the live attempts of one host, at most 8 name theorems whose adapter lies on any one host, and for each block index at most 8 name theorems whose block of that index lies on any one host. One host holds the adapters named by 8 live attempts of every host, and one host holds the first blocks named by 8 live attempts of every host. `host_live_count`: rows at or above a host's count are empty; some host has all 32 rows live. `adapter_pool_row`: all entries differ; pool row p lies on host p. `prefix_pool_row`: all entries differ; pool row p lies on host p // 4.
All inputs are finite; a program needn't handle non-finite values.
Results may differ from a plain program's by a relative error of at most 0.011.
Values may be sent and summed in bfloat16 or wider, within the bound.
No kernel may reach another device: no remote copies, remote signals or barrier semaphores. Data moves between devices by JAX's collectives and lax.ppermute only.
A program may use at most 64 MiB of HBM per device.

v0:
```python
import jax
import jax.numpy as jnp
from jax import lax
from jax.sharding import PartitionSpec as P

HEAD_SIZE = 128
ADAPTER_RANK = 64
BLK = 128
PBLK = 4
ADAPTER_SCALE = 0.5
ROPE_BASE = 10000.0
NEG_FILL = -1e30


def rotate(values, position):
    shaped = values.reshape(values.shape[:-1] + (-1, HEAD_SIZE))
    halfway = HEAD_SIZE // 2
    frequency = ROPE_BASE ** (-(jnp.arange(halfway, dtype=jnp.float32) * (2.0 / HEAD_SIZE)))
    angles = position.astype(jnp.float32)[..., None] * frequency
    cosine = jnp.cos(angles)[..., None, :]
    sine_part = jnp.sin(angles)[..., None, :]
    first_half = shaped[..., :halfway]
    second = shaped[..., halfway:]
    turned = jnp.concatenate(
        [first_half * cosine - second * sine_part, second * cosine + first_half * sine_part],
        axis=-1,
    )
    return turned.reshape(values.shape)


def lookup_table(source_table, wanted):
    matches = wanted[:, None] == jnp.arange(source_table.shape[0], dtype=jnp.int32)[None, :]
    if source_table.ndim == 1:
        return jnp.sum(jnp.where(matches, source_table[None, :], 0), axis=1)
    return jnp.sum(jnp.where(matches[:, :, None], source_table[None, :, :], 0), axis=1)


def route_matrix(destination, validity, capacity, host_total):
    ordinal = jnp.arange(destination.shape[0], dtype=jnp.int32)
    earlier = (
        (destination[:, None] == destination[None, :])
        & validity[None, :]
        & (ordinal[None, :] < ordinal[:, None])
    )
    ranking = jnp.sum(earlier.astype(jnp.int32), axis=1)
    target = destination * capacity + ranking
    places = jnp.arange(host_total * capacity, dtype=jnp.int32)
    return ((places[:, None] == target[None, :]) & validity[None, :]).astype(jnp.bfloat16)


def pack_rows(router, payload):
    return jnp.dot(router, payload, preferred_element_type=jnp.float32).astype(jnp.bfloat16)


def attend_local(queries, chosen, statement_prefix_cache):
    head_count = queries.shape[-1] // HEAD_SIZE
    blocks = statement_prefix_cache.shape[0]
    block_keys = statement_prefix_cache[:, 0].reshape(
        blocks, statement_prefix_cache.shape[2], head_count, HEAD_SIZE
    )
    block_values = statement_prefix_cache[:, 1].reshape(
        blocks, statement_prefix_cache.shape[2], head_count, HEAD_SIZE
    )
    shaped = queries.reshape(queries.shape[:-1] + (head_count, HEAD_SIZE))
    scores = jnp.einsum(
        "nchd,bthd->ncbht", shaped, block_keys, preferred_element_type=jnp.float32
    ) * HEAD_SIZE ** (-0.5)
    chosen_mask = (chosen > 0)[:, :, :, None, None]
    masked = jnp.where(chosen_mask, scores, NEG_FILL)
    top_score = jnp.max(masked, axis=(2, 4))
    weights = jnp.where(chosen_mask, jnp.exp(masked - top_score[:, :, None, :, None]), 0.0)
    totals = jnp.sum(weights, axis=(2, 4))
    mixed_rows = jnp.einsum(
        "ncbht,bthd->nchd",
        weights.astype(jnp.bfloat16),
        block_values,
        preferred_element_type=jnp.float32,
    )
    return (mixed_rows.reshape(queries.shape), top_score, totals)


def body(
    hidden,
    base_query_projection,
    base_key_projection,
    base_value_projection,
    adapter_input_factors,
    adapter_output_factors,
    statement_prefix_cache,
    generated_token_cache,
    attempt_theorem_index,
    host_live_count,
    adapter_pool_row,
    prefix_pool_row,
    prefix_block_count,
):
    host_total = lax.axis_size("hosts")
    attempts = hidden.shape[0]
    capacity = max(1, attempts // host_total)
    owner_held_rows = adapter_input_factors.shape[0]
    local_blocks = statement_prefix_cache.shape[0]
    row_width = base_query_projection.shape[1]
    head_count = row_width // HEAD_SIZE
    ordinal = jnp.arange(attempts, dtype=jnp.int32)
    living = ordinal < host_live_count[0]
    adapter_rows = lookup_table(adapter_pool_row, attempt_theorem_index)
    block_rows = lookup_table(prefix_pool_row, attempt_theorem_index)
    block_counts = lookup_table(prefix_block_count, attempt_theorem_index)
    position = BLK * block_counts + generated_token_cache.shape[2]
    adapter_router = route_matrix(adapter_rows // owner_held_rows, living, capacity, host_total)
    adapter_pick = (
        adapter_rows[:, None] % owner_held_rows
        == jnp.arange(owner_held_rows, dtype=jnp.int32)[None, :]
    ).astype(jnp.bfloat16)
    sent_hidden = pack_rows(adapter_router, hidden).reshape(host_total, capacity, hidden.shape[1])
    sent_pick = pack_rows(adapter_router, adapter_pick).reshape(
        host_total, capacity, owner_held_rows
    )
    incoming_rows = lax.all_to_all(sent_hidden, "hosts", split_axis=0, concat_axis=0, tiled=True)
    pick_in = lax.all_to_all(sent_pick, "hosts", split_axis=0, concat_axis=0, tiled=True)
    projected_rows = jnp.einsum(
        "xjp,epk->xjek", incoming_rows, adapter_input_factors, preferred_element_type=jnp.float32
    )
    partial_rank = jnp.sum(projected_rows * pick_in.astype(jnp.float32)[..., None], axis=2)
    rank_rows = lax.psum(partial_rank, "mp").astype(jnp.bfloat16)
    spread_rows = rank_rows[:, :, None, :] * pick_in[..., None]
    query_correction = jnp.einsum(
        "exqw,qwf->exf",
        spread_rows[..., :ADAPTER_RANK],
        adapter_output_factors[:, 0],
        preferred_element_type=jnp.float32,
    )
    value_correction = jnp.einsum(
        "exqw,qwf->exf",
        spread_rows[..., ADAPTER_RANK:],
        adapter_output_factors[:, 1],
        preferred_element_type=jnp.float32,
    )
    adapter_corrections = (
        jnp.concatenate([query_correction, value_correction], axis=-1) * ADAPTER_SCALE
    ).astype(jnp.bfloat16)
    returned = lax.all_to_all(adapter_corrections, "hosts", split_axis=0, concat_axis=0, tiled=True)
    adapter_corrections = jnp.dot(
        adapter_router.T,
        returned.reshape(host_total * capacity, 2 * row_width),
        preferred_element_type=jnp.float32,
    )
    query_rows = rotate(
        base_query_projection.astype(jnp.float32) + adapter_corrections[:, :row_width], position
    ).astype(jnp.bfloat16)
    value_rows = (
        base_value_projection.astype(jnp.float32) + adapter_corrections[:, row_width:]
    ).astype(jnp.bfloat16)
    key_rows = rotate(base_key_projection.astype(jnp.float32), position).astype(jnp.bfloat16)
    requests = []
    for block_index in range(PBLK):
        wanted = living & (block_index < block_counts)
        holder = block_rows[:, block_index]
        router = route_matrix(holder // local_blocks, wanted, capacity, host_total)
        block_pick = (
            holder[:, None] % local_blocks == jnp.arange(local_blocks, dtype=jnp.int32)[None, :]
        ).astype(jnp.bfloat16)
        sent_queries = pack_rows(router, query_rows).reshape(host_total, capacity, row_width)
        sent_blocks = pack_rows(router, block_pick).reshape(host_total, capacity, local_blocks)
        requests.append((router, wanted, sent_queries, sent_blocks))
    partials = []
    for request in requests:
        answer_mixed_rows, answer_top_score, answer_totals = attend_local(
            lax.all_to_all(request[2], "hosts", split_axis=0, concat_axis=0, tiled=True),
            lax.all_to_all(request[3], "hosts", split_axis=0, concat_axis=0, tiled=True),
            statement_prefix_cache,
        )
        partials.append(
            (
                lax.all_to_all(answer_mixed_rows, "hosts", split_axis=0, concat_axis=0, tiled=True),
                lax.all_to_all(answer_top_score, "hosts", split_axis=0, concat_axis=0, tiled=True),
                lax.all_to_all(answer_totals, "hosts", split_axis=0, concat_axis=0, tiled=True),
            )
        )
    entries = []
    for block_index in range(PBLK):
        router, wanted = (requests[block_index][0], requests[block_index][1])
        mixed_rows, top_score, totals = partials[block_index]
        back_router = router.T.astype(jnp.float32)
        flat_mixed = jnp.dot(
            back_router,
            mixed_rows.reshape(host_total * capacity, row_width),
            precision=lax.Precision.HIGHEST,
        )
        flat_top = jnp.dot(
            back_router,
            top_score.reshape(host_total * capacity, head_count),
            precision=lax.Precision.HIGHEST,
        )
        flat_totals = jnp.dot(
            back_router,
            totals.reshape(host_total * capacity, head_count),
            precision=lax.Precision.HIGHEST,
        )
        flat_top = jnp.where(wanted[:, None], flat_top, NEG_FILL)
        entries.append((flat_mixed, flat_top, flat_totals))
    shaped_query = query_rows.reshape(attempts, head_count, HEAD_SIZE)
    own_keys = jnp.concatenate([generated_token_cache[:, 0], key_rows[:, None, :]], axis=1).reshape(
        attempts, -1, head_count, HEAD_SIZE
    )
    own_values = jnp.concatenate(
        [generated_token_cache[:, 1], value_rows[:, None, :]], axis=1
    ).reshape(attempts, -1, head_count, HEAD_SIZE)
    own_scores = jnp.einsum(
        "ahd,athd->aht", shaped_query, own_keys, preferred_element_type=jnp.float32
    ) * HEAD_SIZE ** (-0.5)
    own_top = jnp.max(own_scores, axis=2)
    own_weights = jnp.exp(own_scores - own_top[..., None])
    own_totals = jnp.sum(own_weights, axis=2)
    own_mixed = jnp.einsum(
        "aht,athd->ahd",
        own_weights.astype(jnp.bfloat16),
        own_values,
        preferred_element_type=jnp.float32,
    )
    overall = own_top
    for flat_mixed, flat_top, flat_totals in entries:
        overall = jnp.maximum(overall, flat_top)
    own_factor = jnp.exp(own_top - overall)
    numerator = own_mixed * own_factor[..., None]
    denominator = own_totals * own_factor
    for flat_mixed, flat_top, flat_totals in entries:
        factor = jnp.exp(flat_top - overall)
        numerator = (
            numerator + flat_mixed.reshape(attempts, head_count, HEAD_SIZE) * factor[..., None]
        )
        denominator = denominator + flat_totals * factor
    attended = (numerator / denominator[..., None]).reshape(attempts, row_width)
    live_rows = living[:, None]
    return (
        jnp.where(live_rows, attended, 0.0).astype(jnp.bfloat16),
        jnp.where(live_rows, key_rows, 0.0),
        jnp.where(live_rows, value_rows, 0.0),
    )


def solution(mesh):
    placed = (
        P(("groups", "hosts"), "mp"),
        P(("groups", "hosts"), "mp"),
        P(("groups", "hosts"), "mp"),
        P(("groups", "hosts"), "mp"),
        P(("groups", "hosts"), "mp", None),
        P(("groups", "hosts"), None, None, "mp"),
        P(("groups", "hosts"), None, None, "mp"),
        P(("groups", "hosts"), None, None, "mp"),
        P(("groups", "hosts")),
        P(("groups", "hosts")),
        P("groups"),
        P("groups", None),
        P("groups"),
    )
    return jax.shard_map(
        body,
        mesh=mesh,
        in_specs=placed,
        out_specs=(
            P(("groups", "hosts"), "mp"),
            P(("groups", "hosts"), "mp"),
            P(("groups", "hosts"), "mp"),
        ),
        check_vma=False,
    )
```

profile of v0, /device:TPU:0, one launch (start us, length us, event | category | flops | bytes accessed | tf_op | source)
XLA Modules:
  0.0 238.8 jit_solution(13844421475531033518)
XLA Ops:
  3.2 6.3 %all-to-all-start.1 = ((bf16[4,8,1]{1,2,0:T(2,128)(2,1)}), bf16[4,8,1]{1,2,0:T(2,128)(2,1)S(1)}, u32[]{:S(2)}, u32[]{:S(2)}) async-start(bf16[4,8,1]{1,2,0:T(2,128)(2,1)} %reshape.598), calls=%async_computation.1 | async-start | bytes 4096 | tf_op jit(solution)/shard_map/all_to_all | solution.py:120
  15.3 1.7 fusion.14
  19.2 1.1 slice_bitcast_fusion
  20.2 1.8 fusion.207
  23.4 5.1 %all-to-all-start.3 = ((bf16[4,8,4]{1,2,0:T(4,128)(2,1)}), bf16[4,8,4]{1,2,0:T(4,128)(2,1)S(1)}, u32[]{:S(2)}, u32[]{:S(2)}) async-start(bf16[4,8,4]{1,2,0:T(4,128)(2,1)} %copy.229), calls=%async_computation.3 | async-start | bytes 8192 | tf_op jit(solution)/shard_map/all_to_all | solution.py:170
  28.5 5.6 %all-to-all-done.3 = bf16[4,8,4]{1,2,0:T(4,128)(2,1)S(1)} async-done(((bf16[4,8,4]{1,2,0:T(4,128)(2,1)}), bf16[4,8,4]{1,2,0:T(4,128)(2,1)S(1)}, u32[]{:S(2)}, u32[]{:S(2)}) %all-to-all-start.3) | async-done | bytes 288 | tf_op jit(solution)/shard_map/all_to_all | solution.py:170
  34.1 3.2 %all-to-all-start.6 = ((bf16[4,8,4]{1,2,0:T(4,128)(2,1)}), bf16[4,8,4]{1,2,0:T(4,128)(2,1)S(1)}, u32[]{:S(2)}, u32[]{:S(2)}) async-start(bf16[4,8,4]{1,2,0:T(4,128)(2,1)} %copy.235), calls=%async_computation.6 | async-start | bytes 8192 | tf_op jit(solution)/shard_map/all_to_all | solution.py:170
  37.9 4.8 %all-to-all-done.6 = bf16[4,8,4]{1,2,0:T(4,128)(2,1)S(1)} async-done(((bf16[4,8,4]{1,2,0:T(4,128)(2,1)}), bf16[4,8,4]{1,2,0:T(4,128)(2,1)S(1)}, u32[]{:S(2)}, u32[]{:S(2)}) %all-to-all-start.6) | async-done | bytes 288 | tf_op jit(solution)/shard_map/all_to_all | solution.py:170
  42.7 3.2 %all-to-all-start.9 = ((bf16[4,8,4]{1,2,0:T(4,128)(2,1)}), bf16[4,8,4]{1,2,0:T(4,128)(2,1)S(1)}, u32[]{:S(2)}, u32[]{:S(2)}) async-start(bf16[4,8,4]{1,2,0:T(4,128)(2,1)} %copy.240), calls=%async_computation.9 | async-start | bytes 8192 | tf_op jit(solution)/shard_map/all_to_all | solution.py:170
  46.6 4.9 %all-to-all-done.9 = bf16[4,8,4]{1,2,0:T(4,128)(2,1)S(1)} async-done(((bf16[4,8,4]{1,2,0:T(4,128)(2,1)}), bf16[4,8,4]{1,2,0:T(4,128)(2,1)S(1)}, u32[]{:S(2)}, u32[]{:S(2)}) %all-to-all-start.9) | async-done | bytes 288 | tf_op jit(solution)/shard_map/all_to_all | solution.py:170
  51.5 3.3 %all-to-all-start = ((bf16[4,8,1024]{2,1,0:T(8,128)(2,1)}), bf16[4,8,1024]{2,1,0:T(8,128)(2,1)S(1)}, u32[]{:S(2)}, u32[]{:S(2)}) async-start(bf16[4,8,1024]{2,1,0:T(8,128)(2,1)} %fusion.14), calls=%async_computation | async-start | bytes 131072 | tf_op jit(solution)/shard_map/all_to_all | solution.py:119
  55.4 5.1 %all-to-all-done = bf16[4,8,1024]{2,1,0:T(8,128)(2,1)S(1)} async-done(((bf16[4,8,1024]{2,1,0:T(8,128)(2,1)}), bf16[4,8,1024]{2,1,0:T(8,128)(2,1)S(1)}, u32[]{:S(2)}, u32[]{:S(2)}) %all-to-all-start) | async-done | bytes 65568 | tf_op jit(solution)/shard_map/all_to_all | solution.py:119
  60.5 3.2 %all-to-all-start.12 = ((bf16[4,8,4]{1,2,0:T(4,128)(2,1)}), bf16[4,8,4]{1,2,0:T(4,128)(2,1)S(1)}, u32[]{:S(2)}, u32[]{:S(2)}) async-start(bf16[4,8,4]{1,2,0:T(4,128)(2,1)} %copy.245), calls=%async_computation.12 | async-start | bytes 8192 | tf_op jit(solution)/shard_map/all_to_all | solution.py:170
  63.9 10.4 %psum.7 = bf16[4,8,128]{2,1,0:T(8,128)(2,1)S(1)} all-reduce(f32[4,8,128]{2,1,0:T(8,128)S(1)} %convolution_multiply_fusion.8), channel_id=1, replica_groups=mesh['groups'=2,'hosts'=4,'mp'=4] {'mp'}, use_global_device_ids=true, to_apply=%region_2.3 | all-reduce | flops 4096 | bytes 24576 | tf_op jit(solution)/shard_map/psum | solution.py:125
  74.4 1.1 fusion.77
  75.5 1.1 fusion.79
  77.2 4.8 %all-to-all-start.2 = ((bf16[4,8,2048]{2,1,0:T(8,128)(2,1)}), bf16[4,8,2048]{2,1,0:T(8,128)(2,1)S(1)}, u32[]{:S(2)}, u32[]{:S(2)}) async-start(bf16[4,8,2048]{2,1,0:T(8,128)(2,1)} %fusion.52), calls=%async_computation.2 | async-start | bytes 262144 | tf_op jit(solution)/shard_map/all_to_all | solution.py:142
  82.6 5.3 %all-to-all-done.2 = bf16[4,8,2048]{2,1,0:T(8,128)(2,1)S(1)} async-done(((bf16[4,8,2048]{2,1,0:T(8,128)(2,1)}), bf16[4,8,2048]{2,1,0:T(8,128)(2,1)S(1)}, u32[]{:S(2)}, u32[]{:S(2)}) %all-to-all-start.2) | async-done | bytes 131104 | tf_op jit(solution)/shard_map/all_to_all | solution.py:142
  88.5 0.9 fusion.18
  89.4 3.3 %all-to-all-start.13 = ((bf16[4,8,1024]{2,1,0:T(8,128)(2,1)}), bf16[4,8,1024]{2,1,0:T(8,128)(2,1)S(1)}, u32[]{:S(2)}, u32[]{:S(2)}) async-start(bf16[4,8,1024]{2,1,0:T(8,128)(2,1)} %fusion.18), calls=%async_computation.13 | async-start | bytes 131072 | tf_op jit(solution)/shard_map/all_to_all | solution.py:169
  92.7 1.6 broadcast_select_fusion
  94.4 1.8 fusion.24
  97.1 1.1 fusion.28
  98.2 0.9 fusion.17
  99.1 5.0 %all-to-all-start.10 = ((bf16[4,8,1024]{2,1,0:T(8,128)(2,1)}), bf16[4,8,1024]{2,1,0:T(8,128)(2,1)S(1)}, u32[]{:S(2)}, u32[]{:S(2)}) async-start(bf16[4,8,1024]{2,1,0:T(8,128)(2,1)} %fusion.17), calls=%async_computation.10 | async-start | bytes 131072 | tf_op jit(solution)/shard_map/all_to_all | solution.py:169
  104.2 0.9 fusion.16
  105.1 4.8 %all-to-all-done.10 = bf16[4,8,1024]{2,1,0:T(8,128)(2,1)S(1)} async-done(((bf16[4,8,1024]{2,1,0:T(8,128)(2,1)}), bf16[4,8,1024]{2,1,0:T(8,128)(2,1)S(1)}, u32[]{:S(2)}, u32[]{:S(2)}) %all-to-all-start.10) | async-done | bytes 65568 | tf_op jit(solution)/shard_map/all_to_all | solution.py:169
  109.9 3.3 %all-to-all-start.7 = ((bf16[4,8,1024]{2,1,0:T(8,128)(2,1)}), bf16[4,8,1024]{2,1,0:T(8,128)(2,1)S(1)}, u32[]{:S(2)}, u32[]{:S(2)}) async-start(bf16[4,8,1024]{2,1,0:T(8,128)(2,1)} %fusion.16), calls=%async_computation.7 | async-start | bytes 131072 | tf_op jit(solution)/shard_map/all_to_all | solution.py:169
  113.2 0.9 fusion.15
  114.2 4.7 %all-to-all-done.7 = bf16[4,8,1024]{2,1,0:T(8,128)(2,1)S(1)} async-done(((bf16[4,8,1024]{2,1,0:T(8,128)(2,1)}), bf16[4,8,1024]{2,1,0:T(8,128)(2,1)S(1)}, u32[]{:S(2)}, u32[]{:S(2)}) %all-to-all-start.7) | async-done | bytes 65568 | tf_op jit(solution)/shard_map/all_to_all | solution.py:169
  118.9 3.3 %all-to-all-start.4 = ((bf16[4,8,1024]{2,1,0:T(8,128)(2,1)}), bf16[4,8,1024]{2,1,0:T(8,128)(2,1)S(1)}, u32[]{:S(2)}, u32[]{:S(2)}) async-start(bf16[4,8,1024]{2,1,0:T(8,128)(2,1)} %fusion.15), calls=%async_computation.4 | async-start | bytes 131072 | tf_op jit(solution)/shard_map/all_to_all | solution.py:169
  123.0 1.0 fusion.208
  124.0 1.1 convolution_bitcast_fusion.2
  125.2 1.1 convolution_bitcast_fusion.1
  127.9 4.3 %all-to-all-start.20 = ((f32[4,8,8]{1,2,0:T(8,128)}), f32[4,8,8]{1,2,0:T(8,128)S(1)}, u32[]{:S(2)}, u32[]{:S(2)}) async-start(f32[4,8,8]{1,2,0:T(8,128)} %copy.265), calls=%async_computation.20 | async-start | bytes 32768 | tf_op jit(solution)/shard_map/all_to_all | solution.py:177
  132.3 1.1 convolution_bitcast_fusion
  133.4 1.3 copy.238
  134.7 3.1 %all-to-all-done.20 = f32[4,8,8]{1,2,0:T(8,128)S(1)} async-done(((f32[4,8,8]{1,2,0:T(8,128)}), f32[4,8,8]{1,2,0:T(8,128)S(1)}, u32[]{:S(2)}, u32[]{:S(2)}) %all-to-all-start.20) | async-done | bytes 1056 | tf_op jit(solution)/shard_map/all_to_all | solution.py:177
  137.9 3.3 %all-to-all-start.8 = ((f32[4,8,8]{1,2,0:T(8,128)}), f32[4,8,8]{1,2,0:T(8,128)S(1)}, u32[]{:S(2)}, u32[]{:S(2)}) async-start(f32[4,8,8]{1,2,0:T(8,128)} %copy.238), calls=%async_computation.8 | async-start | bytes 32768 | tf_op jit(solution)/shard_map/all_to_all | solution.py:176
  141.1 1.0 fusion.44
  142.7 4.0 %all-to-all-done.8 = f32[4,8,8]{1,2,0:T(8,128)S(1)} async-done(((f32[4,8,8]{1,2,0:T(8,128)}), f32[4,8,8]{1,2,0:T(8,128)S(1)}, u32[]{:S(2)}, u32[]{:S(2)}) %all-to-all-start.8) | async-done | bytes 1056 | tf_op jit(solution)/shard_map/all_to_all | solution.py:176
  146.7 3.2 %all-to-all-start.21 = ((f32[4,8,8]{1,2,0:T(8,128)}), f32[4,8,8]{1,2,0:T(8,128)S(1)}, u32[]{:S(2)}, u32[]{:S(2)}) async-start(f32[4,8,8]{1,2,0:T(8,128)} %copy.267), calls=%async_computation.21 | async-start | bytes 32768 | tf_op jit(solution)/shard_map/all_to_all | solution.py:177
  150.0 1.0 fusion.209
  151.7 3.9 %all-to-all-done.21 = f32[4,8,8]{1,2,0:T(8,128)S(1)} async-done(((f32[4,8,8]{1,2,0:T(8,128)}), f32[4,8,8]{1,2,0:T(8,128)S(1)}, u32[]{:S(2)}, u32[]{:S(2)}) %all-to-all-start.21) | async-done | bytes 1056 | tf_op jit(solution)/shard_map/all_to_all | solution.py:177
  155.5 3.3 %all-to-all-start.11 = ((f32[4,8,8]{1,2,0:T(8,128)}), f32[4,8,8]{1,2,0:T(8,128)S(1)}, u32[]{:S(2)}, u32[]{:S(2)}) async-start(f32[4,8,8]{1,2,0:T(8,128)} %copy.243), calls=%async_computation.11 | async-start | bytes 32768 | tf_op jit(solution)/shard_map/all_to_all | solution.py:176
  158.8 0.9 fusion.46
  160.4 4.0 %all-to-all-done.11 = f32[4,8,8]{1,2,0:T(8,128)S(1)} async-done(((f32[4,8,8]{1,2,0:T(8,128)}), f32[4,8,8]{1,2,0:T(8,128)S(1)}, u32[]{:S(2)}, u32[]{:S(2)}) %all-to-all-start.11) | async-done | bytes 1056 | tf_op jit(solution)/shard_map/all_to_all | solution.py:176
  164.4 3.2 %all-to-all-start.22 = ((f32[4,8,8]{1,2,0:T(8,128)}), f32[4,8,8]{1,2,0:T(8,128)S(1)}, u32[]{:S(2)}, u32[]{:S(2)}) async-start(f32[4,8,8]{1,2,0:T(8,128)} %copy.269), calls=%async_computation.22 | async-start | bytes 32768 | tf_op jit(solution)/shard_map/all_to_all | solution.py:177
  167.7 1.1 convolution_bitcast_fusion.3
  169.4 3.8 %all-to-all-done.22 = f32[4,8,8]{1,2,0:T(8,128)S(1)} async-done(((f32[4,8,8]{1,2,0:T(8,128)}), f32[4,8,8]{1,2,0:T(8,128)S(1)}, u32[]{:S(2)}, u32[]{:S(2)}) %all-to-all-start.22) | async-done | bytes 1056 | tf_op jit(solution)/shard_map/all_to_all | solution.py:177
  173.2 3.2 %all-to-all-start.14 = ((f32[4,8,8]{1,2,0:T(8,128)}), f32[4,8,8]{1,2,0:T(8,128)S(1)}, u32[]{:S(2)}, u32[]{:S(2)}) async-start(f32[4,8,8]{1,2,0:T(8,128)} %copy.248), calls=%async_computation.14 | async-start | bytes 32768 | tf_op jit(solution)/shard_map/all_to_all | solution.py:176
  180.7 1.3 all-to-all-done.14
  182.0 3.7 %all-to-all-start.19 = ((f32[4,8,8]{1,2,0:T(8,128)}), f32[4,8,8]{1,2,0:T(8,128)S(1)}, u32[]{:S(2)}, u32[]{:S(2)}) async-start(f32[4,8,8]{1,2,0:T(8,128)} %copy.263), calls=%async_computation.19 | async-start | bytes 32768 | tf_op jit(solution)/shard_map/all_to_all | solution.py:177
  186.1 5.3 %all-to-all-done.19 = f32[4,8,8]{1,2,0:T(8,128)S(1)} async-done(((f32[4,8,8]{1,2,0:T(8,128)}), f32[4,8,8]{1,2,0:T(8,128)S(1)}, u32[]{:S(2)}, u32[]{:S(2)}) %all-to-all-start.19) | async-done | bytes 1056 | tf_op jit(solution)/shard_map/all_to_all | solution.py:177
  191.4 3.3 %all-to-all-start.5 = ((f32[4,8,8]{1,2,0:T(8,128)}), f32[4,8,8]{1,2,0:T(8,128)S(1)}, u32[]{:S(2)}, u32[]{:S(2)}) async-start(f32[4,8,8]{1,2,0:T(8,128)} %copy.233), calls=%async_computation.5 | async-start | bytes 32768 | tf_op jit(solution)/shard_map/all_to_all | solution.py:176
  195.3 4.9 %all-to-all-done.5 = f32[4,8,8]{1,2,0:T(8,128)S(1)} async-done(((f32[4,8,8]{1,2,0:T(8,128)}), f32[4,8,8]{1,2,0:T(8,128)S(1)}, u32[]{:S(2)}, u32[]{:S(2)}) %all-to-all-start.5) | async-done | bytes 1056 | tf_op jit(solution)/shard_map/all_to_all | solution.py:176
  200.2 3.3 %all-to-all-start.16 = ((f32[4,8,1024]{2,1,0:T(8,128)}), f32[4,8,1024]{2,1,0:T(8,128)S(1)}, u32[]{:S(2)}, u32[]{:S(2)}) async-start(f32[4,8,1024]{2,1,0:T(8,128)} %bitcast.311), calls=%async_computation.16 | async-start | bytes 262144 | tf_op jit(solution)/shard_map/all_to_all | solution.py:175
  204.9 4.5 %all-to-all-done.16 = f32[4,8,1024]{2,1,0:T(8,128)S(1)} async-done(((f32[4,8,1024]{2,1,0:T(8,128)}), f32[4,8,1024]{2,1,0:T(8,128)S(1)}, u32[]{:S(2)}, u32[]{:S(2)}) %all-to-all-start.16) | async-done | bytes 131104 | tf_op jit(solution)/shard_map/all_to_all | solution.py:175
  209.4 3.3 %all-to-all-start.17 = ((f32[4,8,1024]{2,1,0:T(8,128)}), f32[4,8,1024]{2,1,0:T(8,128)S(1)}, u32[]{:S(2)}, u32[]{:S(2)}) async-start(f32[4,8,1024]{2,1,0:T(8,128)} %bitcast.310), calls=%async_computation.17 | async-start | bytes 262144 | tf_op jit(solution)/shard_map/all_to_all | solution.py:175
  213.0 6.0 %all-to-all-done.17 = f32[4,8,1024]{2,1,0:T(8,128)S(1)} async-done(((f32[4,8,1024]{2,1,0:T(8,128)}), f32[4,8,1024]{2,1,0:T(8,128)S(1)}, u32[]{:S(2)}, u32[]{:S(2)}) %all-to-all-start.17) | async-done | bytes 131104 | tf_op jit(solution)/shard_map/all_to_all | solution.py:175
  219.0 3.6 %all-to-all-start.18 = ((f32[4,8,1024]{2,1,0:T(8,128)}), f32[4,8,1024]{2,1,0:T(8,128)S(1)}, u32[]{:S(2)}, u32[]{:S(2)}) async-start(f32[4,8,1024]{2,1,0:T(8,128)} %bitcast.309), calls=%async_computation.18 | async-start | bytes 262144 | tf_op jit(solution)/shard_map/all_to_all | solution.py:175
  222.9 5.7 %all-to-all-done.18 = f32[4,8,1024]{2,1,0:T(8,128)S(1)} async-done(((f32[4,8,1024]{2,1,0:T(8,128)}), f32[4,8,1024]{2,1,0:T(8,128)S(1)}, u32[]{:S(2)}, u32[]{:S(2)}) %all-to-all-start.18) | async-done | bytes 131104 | tf_op jit(solution)/shard_map/all_to_all | solution.py:175
  228.5 3.3 %all-to-all-start.15 = ((f32[4,8,1024]{2,1,0:T(8,128)}), f32[4,8,1024]{2,1,0:T(8,128)S(1)}, u32[]{:S(2)}, u32[]{:S(2)}) async-start(f32[4,8,1024]{2,1,0:T(8,128)} %bitcast.312), calls=%async_computation.15 | async-start | bytes 262144 | tf_op jit(solution)/shard_map/all_to_all | solution.py:175
  232.1 5.6 %all-to-all-done.15 = f32[4,8,1024]{2,1,0:T(8,128)S(1)} async-done(((f32[4,8,1024]{2,1,0:T(8,128)}), f32[4,8,1024]{2,1,0:T(8,128)S(1)}, u32[]{:S(2)}, u32[]{:S(2)}) %all-to-all-start.15) | async-done | bytes 131104 | tf_op jit(solution)/shard_map/all_to_all | solution.py:175
  (198 shorter events, 28.8 us)
Async XLA Ops:
  0.6 63.1 %copy-start = (bf16[1,1024,128]{2,1,0:T(8,128)(2,1)S(1)}, bf16[1,1024,128]{2,1,0:T(8,128)(2,1)}, u32[]{:S(2)}) copy-start(bf16[1,1024,128]{2,1,0:T(8,128)(2,1)} %param.17) | copy-start | bytes 786436
  0.6 18.5 %copy-start.1 = (bf16[32,2,8,1024]{3,2,1,0:T(8,128)(2,1)S(1)}, bf16[32,2,8,1024]{3,2,1,0:T(8,128)(2,1)}, u32[]{:S(2)}) copy-start(bf16[32,2,8,1024]{3,2,1,0:T(8,128)(2,1)} %param.20) | copy-start | bytes 3145732
  1.4 91.3 %copy-start.21 = (pred[32]{0:T(512)(128)(4,1)}, pred[32]{0:T(512)(128)(4,1)S(1)}, u32[]{:S(2)}) copy-start(pred[32]{0:T(512)(128)(4,1)S(1)} %iota_compare_fusion.15) | copy-start | bytes 100
  3.2 20.2 %all-to-all-start.1 = ((bf16[4,8,1]{1,2,0:T(2,128)(2,1)}), bf16[4,8,1]{1,2,0:T(2,128)(2,1)S(1)}, u32[]{:S(2)}, u32[]{:S(2)}) async-start(bf16[4,8,1]{1,2,0:T(2,128)(2,1)} %reshape.598), calls=%async_computation.1 | async-start | bytes 4096 | tf_op jit(solution)/shard_map/all_to_all | solution.py:120
  11.0 77.5 %copy-start.23 = (pred[32]{0:T(512)(128)(4,1)}, pred[32]{0:T(512)(128)(4,1)S(1)}, u32[]{:S(2)}) copy-start(pred[32]{0:T(512)(128)(4,1)S(1)} %get-tuple-element.47) | copy-start | bytes 100
  11.1 87.1 %copy-start.25 = (pred[32]{0:T(512)(128)(4,1)}, pred[32]{0:T(512)(128)(4,1)S(1)}, u32[]{:S(2)}) copy-start(pred[32]{0:T(512)(128)(4,1)S(1)} %get-tuple-element.48) | copy-start | bytes 100
  11.1 93.1 %copy-start.27 = (pred[32]{0:T(512)(128)(4,1)}, pred[32]{0:T(512)(128)(4,1)S(1)}, u32[]{:S(2)}) copy-start(pred[32]{0:T(512)(128)(4,1)S(1)} %get-tuple-element.49) | copy-start | bytes 100
  11.1 102.1 %copy-start.29 = (pred[32]{0:T(512)(128)(4,1)}, pred[32]{0:T(512)(128)(4,1)S(1)}, u32[]{:S(2)}) copy-start(pred[32]{0:T(512)(128)(4,1)S(1)} %get-tuple-element.46) | copy-start | bytes 100
  11.2 102.0 %copy-start.38 = (s32[32]{0:T(128)}, s32[32]{0:T(128)S(1)}, u32[]{:S(2)}) copy-start(s32[32]{0:T(128)S(1)} %multiply_add_fusion.4) | copy-start | bytes 388
  11.3 86.9 %copy-start.34 = (s32[32]{0:T(128)}, s32[32]{0:T(128)S(1)}, u32[]{:S(2)}) copy-start(s32[32]{0:T(128)S(1)} %multiply_add_fusion.2) | copy-start | bytes 388
  11.4 92.8 %copy-start.36 = (s32[32]{0:T(128)}, s32[32]{0:T(128)S(1)}, u32[]{:S(2)}) copy-start(s32[32]{0:T(128)S(1)} %multiply_add_fusion.3) | copy-start | bytes 388
  11.5 77.0 %copy-start.32 = (s32[32]{0:T(128)}, s32[32]{0:T(128)S(1)}, u32[]{:S(2)}) copy-start(s32[32]{0:T(128)S(1)} %multiply_add_fusion.1) | copy-start | bytes 388
  23.4 64.8 %copy-start.9 = (bf16[32,1024]{1,0:T(8,128)(2,1)S(1)}, bf16[32,1024]{1,0:T(8,128)(2,1)}, u32[]{:S(2)}) copy-start(bf16[32,1024]{1,0:T(8,128)(2,1)} %param.14) | copy-start | bytes 196612
  23.4 10.7 %all-to-all-start.3 = ((bf16[4,8,4]{1,2,0:T(4,128)(2,1)}), bf16[4,8,4]{1,2,0:T(4,128)(2,1)S(1)}, u32[]{:S(2)}, u32[]{:S(2)}) async-start(bf16[4,8,4]{1,2,0:T(4,128)(2,1)} %copy.229), calls=%async_computation.3 | async-start | bytes 8192 | tf_op jit(solution)/shard_map/all_to_all | solution.py:170
  34.1 8.6 %all-to-all-start.6 = ((bf16[4,8,4]{1,2,0:T(4,128)(2,1)}), bf16[4,8,4]{1,2,0:T(4,128)(2,1)S(1)}, u32[]{:S(2)}, u32[]{:S(2)}) async-start(bf16[4,8,4]{1,2,0:T(4,128)(2,1)} %copy.235), calls=%async_computation.6 | async-start | bytes 8192 | tf_op jit(solution)/shard_map/all_to_all | solution.py:170
  42.7 8.8 %all-to-all-start.9 = ((bf16[4,8,4]{1,2,0:T(4,128)(2,1)}), bf16[4,8,4]{1,2,0:T(4,128)(2,1)S(1)}, u32[]{:S(2)}, u32[]{:S(2)}) async-start(bf16[4,8,4]{1,2,0:T(4,128)(2,1)} %copy.240), calls=%async_computation.9 | async-start | bytes 8192 | tf_op jit(solution)/shard_map/all_to_all | solution.py:170
  51.5 9.0 %all-to-all-start = ((bf16[4,8,1024]{2,1,0:T(8,128)(2,1)}), bf16[4,8,1024]{2,1,0:T(8,128)(2,1)S(1)}, u32[]{:S(2)}, u32[]{:S(2)}) async-start(bf16[4,8,1024]{2,1,0:T(8,128)(2,1)} %fusion.14), calls=%async_computation | async-start | bytes 131072 | tf_op jit(solution)/shard_map/all_to_all | solution.py:119
  60.5 16.7 %all-to-all-start.12 = ((bf16[4,8,4]{1,2,0:T(4,128)(2,1)}), bf16[4,8,4]{1,2,0:T(4,128)(2,1)S(1)}, u32[]{:S(2)}, u32[]{:S(2)}) async-start(bf16[4,8,4]{1,2,0:T(4,128)(2,1)} %copy.245), calls=%async_computation.12 | async-start | bytes 8192 | tf_op jit(solution)/shard_map/all_to_all | solution.py:170
  77.2 10.7 %all-to-all-start.2 = ((bf16[4,8,2048]{2,1,0:T(8,128)(2,1)}), bf16[4,8,2048]{2,1,0:T(8,128)(2,1)S(1)}, u32[]{:S(2)}, u32[]{:S(2)}) async-start(bf16[4,8,2048]{2,1,0:T(8,128)(2,1)} %fusion.52), calls=%async_computation.2 | async-start | bytes 262144 | tf_op jit(solution)/shard_map/all_to_all | solution.py:142
  88.3 8.8 %copy-start.2 = (bf16[32,8,8,128]{3,1,2,0:T(8,128)(2,1)S(1)}, bf16[32,8,8,128]{3,1,2,0:T(8,128)(2,1)}, u32[]{:S(2)}) copy-start(bf16[32,8,8,128]{3,1,2,0:T(8,128)(2,1)} %get-tuple-element.21) | copy-start | bytes 1572868
  89.4 9.7 %all-to-all-start.13 = ((bf16[4,8,1024]{2,1,0:T(8,128)(2,1)}), bf16[4,8,1024]{2,1,0:T(8,128)(2,1)S(1)}, u32[]{:S(2)}, u32[]{:S(2)}) async-start(bf16[4,8,1024]{2,1,0:T(8,128)(2,1)} %fusion.18), calls=%async_computation.13 | async-start | bytes 131072 | tf_op jit(solution)/shard_map/all_to_all | solution.py:169
  96.1 26.1 %copy-start.17 = (pred[4,8,4]{1,2,0:T(4,128)(4,1)S(1)}, pred[4,8,4]{1,2,0:T(4,128)(4,1)}, u32[]{:S(2)}) copy-start(pred[4,8,4]{1,2,0:T(4,128)(4,1)} %broadcast_compare_fusion.2) | copy-start | bytes 388
  96.3 17.8 %copy-start.19 = (f32[32,8]{0,1:T(8,128)}, f32[32,8]{0,1:T(8,128)S(1)}, u32[]{:S(2)}) copy-start(f32[32,8]{0,1:T(8,128)S(1)} %fusion.98) | copy-start | bytes 3076
  98.2 24.4 %copy-start.13 = (pred[4,8,4]{1,2,0:T(4,128)(4,1)S(1)}, pred[4,8,4]{1,2,0:T(4,128)(4,1)}, u32[]{:S(2)}) copy-start(pred[4,8,4]{1,2,0:T(4,128)(4,1)} %broadcast_compare_fusion.1) | copy-start | bytes 388
  99.1 10.8 %all-to-all-start.10 = ((bf16[4,8,1024]{2,1,0:T(8,128)(2,1)}), bf16[4,8,1024]{2,1,0:T(8,128)(2,1)S(1)}, u32[]{:S(2)}, u32[]{:S(2)}) async-start(bf16[4,8,1024]{2,1,0:T(8,128)(2,1)} %fusion.17), calls=%async_computation.10 | async-start | bytes 131072 | tf_op jit(solution)/shard_map/all_to_all | solution.py:169
  109.9 9.0 %all-to-all-start.7 = ((bf16[4,8,1024]{2,1,0:T(8,128)(2,1)}), bf16[4,8,1024]{2,1,0:T(8,128)(2,1)S(1)}, u32[]{:S(2)}, u32[]{:S(2)}) async-start(bf16[4,8,1024]{2,1,0:T(8,128)(2,1)} %fusion.16), calls=%async_computation.7 | async-start | bytes 131072 | tf_op jit(solution)/shard_map/all_to_all | solution.py:169
  118.9 9.0 %all-to-all-start.4 = ((bf16[4,8,1024]{2,1,0:T(8,128)(2,1)}), bf16[4,8,1024]{2,1,0:T(8,128)(2,1)S(1)}, u32[]{:S(2)}, u32[]{:S(2)}) async-start(bf16[4,8,1024]{2,1,0:T(8,128)(2,1)} %fusion.15), calls=%async_computation.4 | async-start | bytes 131072 | tf_op jit(solution)/shard_map/all_to_all | solution.py:169
  122.2 1.8 copy-start.18
  122.6 3.7 %copy-start.5 = (f32[4,8,8]{1,0,2:T(4,128)}, f32[4,8,8]{1,0,2:T(4,128)S(1)}, u32[]{:S(2)}) copy-start(f32[4,8,8]{1,0,2:T(4,128)S(1)} %get-tuple-element.56) | copy-start | bytes 3076
  123.0 3.4 %copy-start.3 = (f32[4,8,8]{1,0,2:T(4,128)}, f32[4,8,8]{1,0,2:T(4,128)S(1)}, u32[]{:S(2)}) copy-start(f32[4,8,8]{1,0,2:T(4,128)S(1)} %get-tuple-element.54) | copy-start | bytes 3076
  123.0 2.2 copy-start.14
  124.0 8.2 %copy-start.16 = (pred[4,8,4]{1,2,0:T(4,128)(4,1)S(1)}, pred[4,8,4]{1,2,0:T(4,128)(4,1)}, u32[]{:S(2)}) copy-start(pred[4,8,4]{1,2,0:T(4,128)(4,1)} %broadcast_compare_fusion) | copy-start | bytes 388
  125.2 16.0 %copy-start.15 = (pred[4,8,4]{1,2,0:T(4,128)(4,1)S(1)}, pred[4,8,4]{1,2,0:T(4,128)(4,1)}, u32[]{:S(2)}) copy-start(pred[4,8,4]{1,2,0:T(4,128)(4,1)} %broadcast_compare_fusion.1) | copy-start | bytes 388
  127.9 10.0 %all-to-all-start.20 = ((f32[4,8,8]{1,2,0:T(8,128)}), f32[4,8,8]{1,2,0:T(8,128)S(1)}, u32[]{:S(2)}, u32[]{:S(2)}) async-start(f32[4,8,8]{1,2,0:T(8,128)} %copy.265), calls=%async_computation.20 | async-start | bytes 32768 | tf_op jit(solution)/shard_map/all_to_all | solution.py:177
  132.3 18.7 %copy-start.4 = (f32[4,8,8]{1,0,2:T(4,128)S(1)}, f32[4,8,8]{1,0,2:T(4,128)}, u32[]{:S(2)}) copy-start(f32[4,8,8]{1,0,2:T(4,128)} %copy-done.3) | copy-start | bytes 3076
  137.9 8.8 %all-to-all-start.8 = ((f32[4,8,8]{1,2,0:T(8,128)}), f32[4,8,8]{1,2,0:T(8,128)S(1)}, u32[]{:S(2)}, u32[]{:S(2)}) async-start(f32[4,8,8]{1,2,0:T(8,128)} %copy.238), calls=%async_computation.8 | async-start | bytes 32768 | tf_op jit(solution)/shard_map/all_to_all | solution.py:176
  146.7 3.3 %copy-start.10 = (f32[4,8,8]{1,2,0:T(8,128)}, f32[4,8,8]{1,2,0:T(8,128)S(1)}, u32[]{:S(2)}) copy-start(f32[4,8,8]{1,2,0:T(8,128)S(1)} %all-to-all-done.8) | copy-start | bytes 3076
  146.7 8.8 %all-to-all-start.21 = ((f32[4,8,8]{1,2,0:T(8,128)}), f32[4,8,8]{1,2,0:T(8,128)S(1)}, u32[]{:S(2)}, u32[]{:S(2)}) async-start(f32[4,8,8]{1,2,0:T(8,128)} %copy.267), calls=%async_computation.21 | async-start | bytes 32768 | tf_op jit(solution)/shard_map/all_to_all | solution.py:177
  151.0 25.4 %copy-start.12 = (pred[4,8,4]{1,2,0:T(4,128)(4,1)S(1)}, pred[4,8,4]{1,2,0:T(4,128)(4,1)}, u32[]{:S(2)}) copy-start(pred[4,8,4]{1,2,0:T(4,128)(4,1)} %broadcast_compare_fusion.3) | copy-start | bytes 388
  151.0 27.6 %copy-start.8 = (f32[8,4,1,8,128]{4,3,2,1,0:T(8,128)S(1)}, f32[8,4,1,8,128]{4,3,2,1,0:T(8,128)}, u32[]{:S(2)}) copy-start(f32[8,4,1,8,128]{4,3,2,1,0:T(8,128)} %convolution_bitcast_fusion) | copy-start | bytes 393220
  151.0 28.2 %copy-start.7 = (f32[8,4,1,8,128]{4,3,2,1,0:T(8,128)S(1)}, f32[8,4,1,8,128]{4,3,2,1,0:T(8,128)}, u32[]{:S(2)}) copy-start(f32[8,4,1,8,128]{4,3,2,1,0:T(8,128)} %convolution_bitcast_fusion.1) | copy-start | bytes 393220
  151.0 28.9 %copy-start.6 = (f32[8,4,1,8,128]{4,3,2,1,0:T(8,128)S(1)}, f32[8,4,1,8,128]{4,3,2,1,0:T(8,128)}, u32[]{:S(2)}) copy-start(f32[8,4,1,8,128]{4,3,2,1,0:T(8,128)} %convolution_bitcast_fusion.2) | copy-start | bytes 393220
  155.5 8.8 %all-to-all-start.11 = ((f32[4,8,8]{1,2,0:T(8,128)}), f32[4,8,8]{1,2,0:T(8,128)S(1)}, u32[]{:S(2)}, u32[]{:S(2)}) async-start(f32[4,8,8]{1,2,0:T(8,128)} %copy.243), calls=%async_computation.11 | async-start | bytes 32768 | tf_op jit(solution)/shard_map/all_to_all | solution.py:176
  158.8 21.8 %copy-start.11 = (f32[4,8,8]{1,2,0:T(8,128)S(1)}, f32[4,8,8]{1,2,0:T(8,128)}, u32[]{:S(2)}) copy-start(f32[4,8,8]{1,2,0:T(8,128)} %copy-done.10) | copy-start | bytes 3076
  158.8 26.9 %copy-start.28 = (pred[32]{0:T(512)(128)(4,1)S(1)}, pred[32]{0:T(512)(128)(4,1)}, u32[]{:S(2)}) copy-start(pred[32]{0:T(512)(128)(4,1)} %copy-done.27) | copy-start | bytes 100
  158.8 26.9 %copy-start.37 = (s32[32]{0:T(128)S(1)}, s32[32]{0:T(128)}, u32[]{:S(2)}) copy-start(s32[32]{0:T(128)} %copy-done.36) | copy-start | bytes 388
  159.8 34.9 %copy-start.26 = (pred[32]{0:T(512)(128)(4,1)S(1)}, pred[32]{0:T(512)(128)(4,1)}, u32[]{:S(2)}) copy-start(pred[32]{0:T(512)(128)(4,1)} %copy-done.25) | copy-start | bytes 100
  159.8 34.9 %copy-start.35 = (s32[32]{0:T(128)S(1)}, s32[32]{0:T(128)}, u32[]{:S(2)}) copy-start(s32[32]{0:T(128)} %copy-done.34) | copy-start | bytes 388
  164.4 8.8 %all-to-all-start.22 = ((f32[4,8,8]{1,2,0:T(8,128)}), f32[4,8,8]{1,2,0:T(8,128)S(1)}, u32[]{:S(2)}, u32[]{:S(2)}) async-start(f32[4,8,8]{1,2,0:T(8,128)} %copy.269), calls=%async_computation.22 | async-start | bytes 32768 | tf_op jit(solution)/shard_map/all_to_all | solution.py:177
  167.6 36.0 %copy-start.30 = (pred[32]{0:T(512)(128)(4,1)S(1)}, pred[32]{0:T(512)(128)(4,1)}, u32[]{:S(2)}) copy-start(pred[32]{0:T(512)(128)(4,1)} %copy-done.29) | copy-start | bytes 100
  167.6 36.0 %copy-start.39 = (s32[32]{0:T(128)S(1)}, s32[32]{0:T(128)}, u32[]{:S(2)}) copy-start(s32[32]{0:T(128)} %copy-done.38) | copy-start | bytes 388
  167.6 36.2 %copy-start.20 = (f32[32,8]{0,1:T(8,128)S(1)}, f32[32,8]{0,1:T(8,128)}, u32[]{:S(2)}) copy-start(f32[32,8]{0,1:T(8,128)} %copy-done.19) | copy-start | bytes 3076
  167.7 36.2 %copy-start.24 = (pred[32]{0:T(512)(128)(4,1)S(1)}, pred[32]{0:T(512)(128)(4,1)}, u32[]{:S(2)}) copy-start(pred[32]{0:T(512)(128)(4,1)} %copy-done.23) | copy-start | bytes 100
  167.7 36.2 %copy-start.33 = (s32[32]{0:T(128)S(1)}, s32[32]{0:T(128)}, u32[]{:S(2)}) copy-start(s32[32]{0:T(128)} %copy-done.32) | copy-start | bytes 388
  167.7 36.4 %copy-start.31 = (f32[32,8]{0,1:T(8,128)S(1)}, f32[32,8]{0,1:T(8,128)}, u32[]{:S(2)}) copy-start(f32[32,8]{0,1:T(8,128)} %get-tuple-element.27) | copy-start | bytes 3076
  173.2 8.8 %all-to-all-start.14 = ((f32[4,8,8]{1,2,0:T(8,128)}), f32[4,8,8]{1,2,0:T(8,128)S(1)}, u32[]{:S(2)}, u32[]{:S(2)}) async-start(f32[4,8,8]{1,2,0:T(8,128)} %copy.248), calls=%async_computation.14 | async-start | bytes 32768 | tf_op jit(solution)/shard_map/all_to_all | solution.py:176
  178.6 59.1 %copy-start.40 = (f32[32,8,1,128]{3,2,1,0:T(1,128)S(1)}, f32[32,8,1,128]{3,2,1,0:T(1,128)}, u32[]{:S(2)}) copy-start(f32[32,8,1,128]{3,2,1,0:T(1,128)} %fusion.28) | copy-start | bytes 393220
  180.6 57.4 %copy-start.22 = (pred[32]{0:T(512)(128)(4,1)S(1)}, pred[32]{0:T(512)(128)(4,1)}, u32[]{:S(2)}) copy-start(pred[32]{0:T(512)(128)(4,1)} %copy-done.21) | copy-start | bytes 100
  182.0 9.3 %all-to-all-start.19 = ((f32[4,8,8]{1,2,0:T(8,128)}), f32[4,8,8]{1,2,0:T(8,128)S(1)}, u32[]{:S(2)}, u32[]{:S(2)}) async-start(f32[4,8,8]{1,2,0:T(8,128)} %copy.263), calls=%async_computation.19 | async-start | bytes 32768 | tf_op jit(solution)/shard_map/all_to_all | solution.py:177
  191.4 8.8 %all-to-all-start.5 = ((f32[4,8,8]{1,2,0:T(8,128)}), f32[4,8,8]{1,2,0:T(8,128)S(1)}, u32[]{:S(2)}, u32[]{:S(2)}) async-start(f32[4,8,8]{1,2,0:T(8,128)} %copy.233), calls=%async_computation.5 | async-start | bytes 32768 | tf_op jit(solution)/shard_map/all_to_all | solution.py:176
  200.2 9.2 %all-to-all-start.16 = ((f32[4,8,1024]{2,1,0:T(8,128)}), f32[4,8,1024]{2,1,0:T(8,128)S(1)}, u32[]{:S(2)}, u32[]{:S(2)}) async-start(f32[4,8,1024]{2,1,0:T(8,128)} %bitcast.311), calls=%async_computation.16 | async-start | bytes 262144 | tf_op jit(solution)/shard_map/all_to_all | solution.py:175
  209.4 9.6 %all-to-all-start.17 = ((f32[4,8,1024]{2,1,0:T(8,128)}), f32[4,8,1024]{2,1,0:T(8,128)S(1)}, u32[]{:S(2)}, u32[]{:S(2)}) async-start(f32[4,8,1024]{2,1,0:T(8,128)} %bitcast.310), calls=%async_computation.17 | async-start | bytes 262144 | tf_op jit(solution)/shard_map/all_to_all | solution.py:175
  219.0 9.5 %all-to-all-start.18 = ((f32[4,8,1024]{2,1,0:T(8,128)}), f32[4,8,1024]{2,1,0:T(8,128)S(1)}, u32[]{:S(2)}, u32[]{:S(2)}) async-start(f32[4,8,1024]{2,1,0:T(8,128)} %bitcast.309), calls=%async_computation.18 | async-start | bytes 262144 | tf_op jit(solution)/shard_map/all_to_all | solution.py:175
  228.5 9.2 %all-to-all-start.15 = ((f32[4,8,1024]{2,1,0:T(8,128)}), f32[4,8,1024]{2,1,0:T(8,128)S(1)}, u32[]{:S(2)}, u32[]{:S(2)}) async-start(f32[4,8,1024]{2,1,0:T(8,128)} %bitcast.312), calls=%async_computation.15 | async-start | bytes 262144 | tf_op jit(solution)/shard_map/all_to_all | solution.py:175
where the time goes:
time: 241 us; the launch traced here: 239 us
  waiting for transfers between devices  88.2 us (37%)
  starting transfers between devices  85.2 us (35%)
  matrix products  21.9 us (9%)
  local copies, waits for them, and re-layouts  18 us (7%)
  other arithmetic  12.8 us (5%)
  blocking collectives  10.4 us (4%)
    all_to_all x4, waiting for transfers between devices, body(): lax.all_to_all(answer_mixed_rows, 'hosts', split_axis=0, concat_axis=0, t...  21.8 us
    all_to_all x4, waiting for transfers between devices, body(): lax.all_to_all(answer_totals, 'hosts', split_axis=0, concat_axis=0, tiled...  16.1 us
    all_to_all x4, waiting for transfers between devices, body(): lax.all_to_all(request[3], 'hosts', split_axis=0, concat_axis=0, tiled=True)  15.3 us
    all_to_all x4, starting transfers between devices, body(): lax.all_to_all(request[2], 'hosts', split_axis=0, concat_axis=0, tiled=True)  14.9 us
    all_to_all x4, starting transfers between devices, body(): lax.all_to_all(request[3], 'hosts', split_axis=0, concat_axis=0, tiled=True)  14.8 us
    all_to_all x4, starting transfers between devices, body(): lax.all_to_all(answer_totals, 'hosts', split_axis=0, concat_axis=0, tiled...  14.5 us
    all_to_all x4, waiting for transfers between devices, body(): lax.all_to_all(answer_top_score, 'hosts', split_axis=0, concat_axis=0, ti...  14.2 us
    all_to_all x4, starting transfers between devices, body(): lax.all_to_all(answer_mixed_rows, 'hosts', split_axis=0, concat_axis=0, t...  13.5 us
  transfers between devices with their start and end apart: 23, of which 20 were waited for; matrix products, arithmetic and copies ran while one was open for 20% of the time, Pallas kernels for 0%

commit v1 on v0

--- a/solution.py
+++ b/solution.py
@@ -10,6 +10,22 @@
 ADAPTER_SCALE = 0.5
 ROPE_BASE = 10000.0
 NEG_FILL = -1e30
+
+
+def exchange_in_pairs(shard, axis, split, join):
+    ways, here = (lax.axis_size(axis), lax.axis_index(axis))
+    width = shard.shape[split] // ways
+    dims = list(shard.shape)
+    dims[split] = width
+    height = dims[join]
+    dims[join] = height * ways
+    full = jnp.zeros(dims, shard.dtype)
+    for mask in range(ways):
+        part = lax.dynamic_slice_in_dim(shard, (here ^ mask) * width, width, axis=split)
+        if mask:
+            part = lax.ppermute(part, axis, [(d, d ^ mask) for d in range(ways)])
+        full = lax.dynamic_update_slice_in_dim(full, part, (here ^ mask) * height, axis=join)
+    return full
 
 
 def rotate(values, position):
@@ -174,7 +190,7 @@
             (
                 lax.all_to_all(answer_mixed_rows, "hosts", split_axis=0, concat_axis=0, tiled=True),
                 lax.all_to_all(answer_top_score, "hosts", split_axis=0, concat_axis=0, tiled=True),
-                lax.all_to_all(answer_totals, "hosts", split_axis=0, concat_axis=0, tiled=True),
+                exchange_in_pairs(answer_totals, "hosts", 0, 0),
             )
         )
     entries = []

time: 241 us -> 221 us (0.917)
  waiting for transfers between devices: 88.2 us -> 75.9 us
  starting transfers between devices: 85.2 us -> 92.3 us
  matrix products: 21.9 us -> 15 us
  other arithmetic: 12.8 us -> 7.94 us
    ppermute x0 -> x12, starting transfers between devices: none -> 18.7 us  [exchange_in_pairs(): part = lax.ppermute(part, axis, [(d, d ^ mask) for d in range(ways)])]
    all_to_all x4 -> x0, waiting for transfers between devices: 16.1 us -> none  [body(): lax.all_to_all(answer_totals, 'hosts', split_axis=0, concat_axis=0, tiled...]
    all_to_all x4 -> x0, starting transfers between devices: 14.5 us -> none  [body(): lax.all_to_all(answer_totals, 'hosts', split_axis=0, concat_axis=0, tiled...]
    all_to_all x4, starting transfers between devices: 13 us -> 17.8 us  [body(): lax.all_to_all(answer_top_score, 'hosts', split_axis=0, concat_axis=0, ti...]
    all_to_all x4, waiting for transfers between devices: 14.2 us -> 10.6 us  [body(): lax.all_to_all(answer_top_score, 'hosts', split_axis=0, concat_axis=0, ti...]
    all_to_all x4, waiting for transfers between devices: 10.3 us -> 13.8 us  [body(): lax.all_to_all(request[2], 'hosts', split_axis=0, concat_axis=0, tiled=True)]
    dot_general x4, matrix products: 4.56 us -> 1.89 us  [attend_local(): jnp.einsum('ncbht,bthd->nchd', weights.astype(jnp.bfloat16), block_values...]
    reduce_sum x4 -> x0, local copies, waits for them, and re-layouts: 2.43 us -> none  [attend_local(): totals = jnp.sum(weights, axis=(2, 4))]
  transfers between devices with their start and end apart: 23 -> 31, of which waited for: 20 -> 16; matrix products, arithmetic and copies ran while one was open for 20% -> 14% of each run, Pallas kernels for 0% -> 0%
where the time goes in v1:
time: 221 us; the launch traced here: 220 us
  starting transfers between devices  92.3 us (42%)
  waiting for transfers between devices  75.9 us (34%)
  local copies, waits for them, and re-layouts  16 us (7%)
  matrix products  15 us (7%)
  blocking collectives  10.4 us (5%)
  other arithmetic  7.94 us (4%)
    all_to_all x4, waiting for transfers between devices, body(): lax.all_to_all(answer_mixed_rows, 'hosts', split_axis=0, concat_axis=0, t...  22 us
    ppermute x12, starting transfers between devices, exchange_in_pairs(): part = lax.ppermute(part, axis, [(d, d ^ mask) for d in range(ways)])  18.7 us
    all_to_all x4, starting transfers between devices, body(): lax.all_to_all(answer_top_score, 'hosts', split_axis=0, concat_axis=0, ti...  17.8 us
    all_to_all x4, waiting for transfers between devices, body(): lax.all_to_all(request[3], 'hosts', split_axis=0, concat_axis=0, tiled=True)  16.5 us
    all_to_all x4, starting transfers between devices, body(): lax.all_to_all(request[3], 'hosts', split_axis=0, concat_axis=0, tiled=True)  14.9 us
    all_to_all x4, waiting for transfers between devices, body(): lax.all_to_all(request[2], 'hosts', split_axis=0, concat_axis=0, tiled=True)  13.8 us
    all_to_all x4, starting transfers between devices, body(): lax.all_to_all(answer_mixed_rows, 'hosts', split_axis=0, concat_axis=0, t...  13.3 us
    all_to_all x4, starting transfers between devices, body(): lax.all_to_all(request[2], 'hosts', split_axis=0, concat_axis=0, tiled=True)  13.1 us
  transfers between devices with their start and end apart: 31, of which 16 were waited for; matrix products, arithmetic and copies ran while one was open for 14% of the time, Pallas kernels for 0%

profile of v1, /device:TPU:0, one launch (start us, length us, event | category | flops | bytes accessed | tf_op | source)
XLA Modules:
  0.0 219.6 jit_solution(1898454604206502019)
XLA Ops:
  1.3 0.8 select_reduce_fusion.2
  2.4 0.7 reshape.598
  3.1 6.3 %all-to-all-start.1 = ((bf16[4,8,1]{1,2,0:T(2,128)(2,1)}), bf16[4,8,1]{1,2,0:T(2,128)(2,1)S(1)}, u32[]{:S(2)}, u32[]{:S(2)}) async-start(bf16[4,8,1]{1,2,0:T(2,128)(2,1)} %reshape.598), calls=%async_computation.1 | async-start | bytes 4096 | tf_op jit(solution)/shard_map/all_to_all | solution.py:136
  10.0 0.7 iota_compare_fusion.14
  10.7 0.8 select_reduce_fusion
  11.5 1.8 fusion.14
  14.9 1.8 fusion.207
  16.8 0.7 copy.258
  17.5 1.3 copy.259
  22.4 0.8 copy.176
  23.2 0.9 slice_bitcast_fusion
  24.1 5.2 %all-to-all-start.3 = ((bf16[4,8,4]{1,2,0:T(4,128)(2,1)}), bf16[4,8,4]{1,2,0:T(4,128)(2,1)S(1)}, u32[]{:S(2)}, u32[]{:S(2)}) async-start(bf16[4,8,4]{1,2,0:T(4,128)(2,1)} %copy.178), calls=%async_computation.3 | async-start | bytes 8192 | tf_op jit(solution)/shard_map/all_to_all | solution.py:186
  29.3 5.6 %all-to-all-done.3 = bf16[4,8,4]{1,2,0:T(4,128)(2,1)S(1)} async-done(((bf16[4,8,4]{1,2,0:T(4,128)(2,1)}), bf16[4,8,4]{1,2,0:T(4,128)(2,1)S(1)}, u32[]{:S(2)}, u32[]{:S(2)}) %all-to-all-start.3) | async-done | bytes 288 | tf_op jit(solution)/shard_map/all_to_all | solution.py:186
  34.9 3.2 %all-to-all-start.6 = ((bf16[4,8,4]{1,2,0:T(4,128)(2,1)}), bf16[4,8,4]{1,2,0:T(4,128)(2,1)S(1)}, u32[]{:S(2)}, u32[]{:S(2)}) async-start(bf16[4,8,4]{1,2,0:T(4,128)(2,1)} %copy.184), calls=%async_computation.6 | async-start | bytes 8192 | tf_op jit(solution)/shard_map/all_to_all | solution.py:186
  38.1 5.4 %all-to-all-done.6 = bf16[4,8,4]{1,2,0:T(4,128)(2,1)S(1)} async-done(((bf16[4,8,4]{1,2,0:T(4,128)(2,1)}), bf16[4,8,4]{1,2,0:T(4,128)(2,1)S(1)}, u32[]{:S(2)}, u32[]{:S(2)}) %all-to-all-start.6) | async-done | bytes 288 | tf_op jit(solution)/shard_map/all_to_all | solution.py:186
  43.5 3.2 %all-to-all-start.9 = ((bf16[4,8,4]{1,2,0:T(4,128)(2,1)}), bf16[4,8,4]{1,2,0:T(4,128)(2,1)S(1)}, u32[]{:S(2)}, u32[]{:S(2)}) async-start(bf16[4,8,4]{1,2,0:T(4,128)(2,1)} %copy.189), calls=%async_computation.9 | async-start | bytes 8192 | tf_op jit(solution)/shard_map/all_to_all | solution.py:186
  46.8 5.5 %all-to-all-done.9 = bf16[4,8,4]{1,2,0:T(4,128)(2,1)S(1)} async-done(((bf16[4,8,4]{1,2,0:T(4,128)(2,1)}), bf16[4,8,4]{1,2,0:T(4,128)(2,1)S(1)}, u32[]{:S(2)}, u32[]{:S(2)}) %all-to-all-start.9) | async-done | bytes 288 | tf_op jit(solution)/shard_map/all_to_all | solution.py:186
  52.3 3.3 %all-to-all-start = ((bf16[4,8,1024]{2,1,0:T(8,128)(2,1)}), bf16[4,8,1024]{2,1,0:T(8,128)(2,1)S(1)}, u32[]{:S(2)}, u32[]{:S(2)}) async-start(bf16[4,8,1024]{2,1,0:T(8,128)(2,1)} %fusion.14), calls=%async_computation | async-start | bytes 131072 | tf_op jit(solution)/shard_map/all_to_all | solution.py:135
  55.6 5.7 %all-to-all-done = bf16[4,8,1024]{2,1,0:T(8,128)(2,1)S(1)} async-done(((bf16[4,8,1024]{2,1,0:T(8,128)(2,1)}), bf16[4,8,1024]{2,1,0:T(8,128)(2,1)S(1)}, u32[]{:S(2)}, u32[]{:S(2)}) %all-to-all-start) | async-done | bytes 65568 | tf_op jit(solution)/shard_map/all_to_all | solution.py:135
  61.3 3.2 %all-to-all-start.12 = ((bf16[4,8,4]{1,2,0:T(4,128)(2,1)}), bf16[4,8,4]{1,2,0:T(4,128)(2,1)S(1)}, u32[]{:S(2)}, u32[]{:S(2)}) async-start(bf16[4,8,4]{1,2,0:T(4,128)(2,1)} %copy.194), calls=%async_computation.12 | async-start | bytes 8192 | tf_op jit(solution)/shard_map/all_to_all | solution.py:186
  64.7 10.4 %psum.7 = bf16[4,8,128]{2,1,0:T(8,128)(2,1)S(1)} all-reduce(f32[4,8,128]{2,1,0:T(8,128)S(1)} %convolution_multiply_fusion.8), channel_id=1, replica_groups=mesh['groups'=2,'hosts'=4,'mp'=4] {'mp'}, use_global_device_ids=true, to_apply=%region_2.3 | all-reduce | flops 4096 | bytes 24576 | tf_op jit(solution)/shard_map/psum | solution.py:141
  75.6 0.7 fusion.52
  76.3 4.8 %all-to-all-start.2 = ((bf16[4,8,2048]{2,1,0:T(8,128)(2,1)}), bf16[4,8,2048]{2,1,0:T(8,128)(2,1)S(1)}, u32[]{:S(2)}, u32[]{:S(2)}) async-start(bf16[4,8,2048]{2,1,0:T(8,128)(2,1)} %fusion.52), calls=%async_computation.2 | async-start | bytes 262144 | tf_op jit(solution)/shard_map/all_to_all | solution.py:158
  81.0 5.9 %all-to-all-done.2 = bf16[4,8,2048]{2,1,0:T(8,128)(2,1)S(1)} async-done(((bf16[4,8,2048]{2,1,0:T(8,128)(2,1)}), bf16[4,8,2048]{2,1,0:T(8,128)(2,1)S(1)}, u32[]{:S(2)}, u32[]{:S(2)}) %all-to-all-start.2) | async-done | bytes 131104 | tf_op jit(solution)/shard_map/all_to_all | solution.py:158
  87.5 0.9 fusion.15
  88.4 0.9 fusion.16
  89.3 0.9 fusion.17
  90.3 3.3 %all-to-all-start.4 = ((bf16[4,8,1024]{2,1,0:T(8,128)(2,1)}), bf16[4,8,1024]{2,1,0:T(8,128)(2,1)S(1)}, u32[]{:S(2)}, u32[]{:S(2)}) async-start(bf16[4,8,1024]{2,1,0:T(8,128)(2,1)} %fusion.15), calls=%async_computation.4 | async-start | bytes 131072 | tf_op jit(solution)/shard_map/all_to_all | solution.py:185
  94.7 0.7 broadcast_select_fusion
  95.5 1.1 fusion.28
  96.5 0.9 fusion.18
  97.4 1.9 all-to-all-done.4
  99.3 3.3 %all-to-all-start.7 = ((bf16[4,8,1024]{2,1,0:T(8,128)(2,1)}), bf16[4,8,1024]{2,1,0:T(8,128)(2,1)S(1)}, u32[]{:S(2)}, u32[]{:S(2)}) async-start(bf16[4,8,1024]{2,1,0:T(8,128)(2,1)} %fusion.16), calls=%async_computation.7 | async-start | bytes 131072 | tf_op jit(solution)/shard_map/all_to_all | solution.py:185
  104.4 4.0 %all-to-all-done.7 = bf16[4,8,1024]{2,1,0:T(8,128)(2,1)S(1)} async-done(((bf16[4,8,1024]{2,1,0:T(8,128)(2,1)}), bf16[4,8,1024]{2,1,0:T(8,128)(2,1)S(1)}, u32[]{:S(2)}, u32[]{:S(2)}) %all-to-all-start.7) | async-done | bytes 65568 | tf_op jit(solution)/shard_map/all_to_all | solution.py:185
  108.3 3.3 %all-to-all-start.10 = ((bf16[4,8,1024]{2,1,0:T(8,128)(2,1)}), bf16[4,8,1024]{2,1,0:T(8,128)(2,1)S(1)}, u32[]{:S(2)}, u32[]{:S(2)}) async-start(bf16[4,8,1024]{2,1,0:T(8,128)(2,1)} %fusion.17), calls=%async_computation.10 | async-start | bytes 131072 | tf_op jit(solution)/shard_map/all_to_all | solution.py:185
  113.3 4.0 %all-to-all-done.10 = bf16[4,8,1024]{2,1,0:T(8,128)(2,1)S(1)} async-done(((bf16[4,8,1024]{2,1,0:T(8,128)(2,1)}), bf16[4,8,1024]{2,1,0:T(8,128)(2,1)S(1)}, u32[]{:S(2)}, u32[]{:S(2)}) %all-to-all-start.10) | async-done | bytes 65568 | tf_op jit(solution)/shard_map/all_to_all | solution.py:185
  117.3 3.3 %all-to-all-start.13 = ((bf16[4,8,1024]{2,1,0:T(8,128)(2,1)}), bf16[4,8,1024]{2,1,0:T(8,128)(2,1)S(1)}, u32[]{:S(2)}, u32[]{:S(2)}) async-start(bf16[4,8,1024]{2,1,0:T(8,128)(2,1)} %fusion.18), calls=%async_computation.13 | async-start | bytes 131072 | tf_op jit(solution)/shard_map/all_to_all | solution.py:185
  122.3 4.0 %all-to-all-done.13 = bf16[4,8,1024]{2,1,0:T(8,128)(2,1)S(1)} async-done(((bf16[4,8,1024]{2,1,0:T(8,128)(2,1)}), bf16[4,8,1024]{2,1,0:T(8,128)(2,1)S(1)}, u32[]{:S(2)}, u32[]{:S(2)}) %all-to-all-start.13) | async-done | bytes 65568 | tf_op jit(solution)/shard_map/all_to_all | solution.py:185
  128.0 0.7 copy.367
  128.7 1.0 collective-permute-start
  130.1 3.1 %collective-permute-start.2 = (f32[1,8,8]{1,0,2:T(1,128)S(1)}, f32[1,8,8]{1,0,2:T(1,128)S(1)}, u32[]{:S(2)}, u32[]{:S(2)}) collective-permute-start(f32[1,8,8]{1,0,2:T(1,128)S(1)} %get-tuple-element.29), channel_id=1, source_target_pairs={{0,12},{4,8},{8,4},{12,0},{1,13},{5,9},{9,5},{13,1},{2,14},{6,10},... | collective-permute-start | bytes 776 | tf_op jit(solution)/shard_map/ppermute | solution.py:26
  133.3 1.3 collective-permute-start.4
  134.6 4.4 %all-to-all-start.11 = ((f32[4,8,8]{1,2,0:T(8,128)}), f32[4,8,8]{1,2,0:T(8,128)S(1)}, u32[]{:S(2)}, u32[]{:S(2)}) async-start(f32[4,8,8]{1,2,0:T(8,128)} %copy.192), calls=%async_computation.11 | async-start | bytes 32768 | tf_op jit(solution)/shard_map/all_to_all | solution.py:192
  139.0 0.7 copy.366
  139.7 0.7 copy.365
  140.3 0.7 copy.364
  141.2 3.9 %collective-permute-start.5 = (f32[1,8,8]{1,0,2:T(1,128)S(1)}, f32[1,8,8]{1,0,2:T(1,128)S(1)}, u32[]{:S(2)}, u32[]{:S(2)}) collective-permute-start(f32[1,8,8]{1,0,2:T(1,128)S(1)} %get-tuple-element.33), channel_id=1, source_target_pairs={{0,12},{4,8},{8,4},{12,0},{1,13},{5,9},{9,5},{13,1},{2,14},{6,10},... | collective-permute-start | bytes 776 | tf_op jit(solution)/shard_map/ppermute | solution.py:26
  146.0 5.1 %all-to-all-start.8 = ((f32[4,8,8]{1,2,0:T(8,128)}), f32[4,8,8]{1,2,0:T(8,128)S(1)}, u32[]{:S(2)}, u32[]{:S(2)}) async-start(f32[4,8,8]{1,2,0:T(8,128)} %copy.187), calls=%async_computation.8 | async-start | bytes 32768 | tf_op jit(solution)/shard_map/all_to_all | solution.py:192
  151.1 3.8 %collective-permute-start.8 = (f32[1,8,8]{1,0,2:T(1,128)S(1)}, f32[1,8,8]{1,0,2:T(1,128)S(1)}, u32[]{:S(2)}, u32[]{:S(2)}) collective-permute-start(f32[1,8,8]{1,0,2:T(1,128)S(1)} %get-tuple-element.37), channel_id=1, source_target_pairs={{0,12},{4,8},{8,4},{12,0},{1,13},{5,9},{9,5},{13,1},{2,14},{6,10},... | collective-permute-start | bytes 776 | tf_op jit(solution)/shard_map/ppermute | solution.py:26
  155.9 3.8 %collective-permute-start.11 = (f32[1,8,8]{1,0,2:T(1,128)S(1)}, f32[1,8,8]{1,0,2:T(1,128)S(1)}, u32[]{:S(2)}, u32[]{:S(2)}) collective-permute-start(f32[1,8,8]{1,0,2:T(1,128)S(1)} %get-tuple-element.41), channel_id=1, source_target_pairs={{0,12},{4,8},{8,4},{12,0},{1,13},{5,9},{9,5},{13,1},{2,14},{6,10},... | collective-permute-start | bytes 776 | tf_op jit(solution)/shard_map/ppermute | solution.py:26
  160.0 1.3 collective-permute-done.11
  161.5 5.1 %all-to-all-start.14 = ((f32[4,8,8]{1,2,0:T(8,128)}), f32[4,8,8]{1,2,0:T(8,128)S(1)}, u32[]{:S(2)}, u32[]{:S(2)}) async-start(f32[4,8,8]{1,2,0:T(8,128)} %copy.197), calls=%async_computation.14 | async-start | bytes 32768 | tf_op jit(solution)/shard_map/all_to_all | solution.py:192
  166.9 5.3 %all-to-all-done.14 = f32[4,8,8]{1,2,0:T(8,128)S(1)} async-done(((f32[4,8,8]{1,2,0:T(8,128)}), f32[4,8,8]{1,2,0:T(8,128)S(1)}, u32[]{:S(2)}, u32[]{:S(2)}) %all-to-all-start.14) | async-done | bytes 1056 | tf_op jit(solution)/shard_map/all_to_all | solution.py:192
  172.2 3.3 %all-to-all-start.5 = ((f32[4,8,8]{1,2,0:T(8,128)}), f32[4,8,8]{1,2,0:T(8,128)S(1)}, u32[]{:S(2)}, u32[]{:S(2)}) async-start(f32[4,8,8]{1,2,0:T(8,128)} %copy.182), calls=%async_computation.5 | async-start | bytes 32768 | tf_op jit(solution)/shard_map/all_to_all | solution.py:192
  175.7 5.3 %all-to-all-done.5 = f32[4,8,8]{1,2,0:T(8,128)S(1)} async-done(((f32[4,8,8]{1,2,0:T(8,128)}), f32[4,8,8]{1,2,0:T(8,128)S(1)}, u32[]{:S(2)}, u32[]{:S(2)}) %all-to-all-start.5) | async-done | bytes 1056 | tf_op jit(solution)/shard_map/all_to_all | solution.py:192
  181.0 3.3 %all-to-all-start.16 = ((f32[4,8,1024]{2,1,0:T(8,128)}), f32[4,8,1024]{2,1,0:T(8,128)S(1)}, u32[]{:S(2)}, u32[]{:S(2)}) async-start(f32[4,8,1024]{2,1,0:T(8,128)} %bitcast.311), calls=%async_computation.16 | async-start | bytes 262144 | tf_op jit(solution)/shard_map/all_to_all | solution.py:191
  185.7 4.5 %all-to-all-done.16 = f32[4,8,1024]{2,1,0:T(8,128)S(1)} async-done(((f32[4,8,1024]{2,1,0:T(8,128)}), f32[4,8,1024]{2,1,0:T(8,128)S(1)}, u32[]{:S(2)}, u32[]{:S(2)}) %all-to-all-start.16) | async-done | bytes 131104 | tf_op jit(solution)/shard_map/all_to_all | solution.py:191
  190.3 3.3 %all-to-all-start.17 = ((f32[4,8,1024]{2,1,0:T(8,128)}), f32[4,8,1024]{2,1,0:T(8,128)S(1)}, u32[]{:S(2)}, u32[]{:S(2)}) async-start(f32[4,8,1024]{2,1,0:T(8,128)} %bitcast.310), calls=%async_computation.17 | async-start | bytes 262144 | tf_op jit(solution)/shard_map/all_to_all | solution.py:191
  193.9 6.2 %all-to-all-done.17 = f32[4,8,1024]{2,1,0:T(8,128)S(1)} async-done(((f32[4,8,1024]{2,1,0:T(8,128)}), f32[4,8,1024]{2,1,0:T(8,128)S(1)}, u32[]{:S(2)}, u32[]{:S(2)}) %all-to-all-start.17) | async-done | bytes 131104 | tf_op jit(solution)/shard_map/all_to_all | solution.py:191
  200.1 3.4 %all-to-all-start.18 = ((f32[4,8,1024]{2,1,0:T(8,128)}), f32[4,8,1024]{2,1,0:T(8,128)S(1)}, u32[]{:S(2)}, u32[]{:S(2)}) async-start(f32[4,8,1024]{2,1,0:T(8,128)} %bitcast.309), calls=%async_computation.18 | async-start | bytes 262144 | tf_op jit(solution)/shard_map/all_to_all | solution.py:191
  203.7 5.7 %all-to-all-done.18 = f32[4,8,1024]{2,1,0:T(8,128)S(1)} async-done(((f32[4,8,1024]{2,1,0:T(8,128)}), f32[4,8,1024]{2,1,0:T(8,128)S(1)}, u32[]{:S(2)}, u32[]{:S(2)}) %all-to-all-start.18) | async-done | bytes 131104 | tf_op jit(solution)/shard_map/all_to_all | solution.py:191
  209.4 3.3 %all-to-all-start.15 = ((f32[4,8,1024]{2,1,0:T(8,128)}), f32[4,8,1024]{2,1,0:T(8,128)S(1)}, u32[]{:S(2)}, u32[]{:S(2)}) async-start(f32[4,8,1024]{2,1,0:T(8,128)} %bitcast.312), calls=%async_computation.15 | async-start | bytes 262144 | tf_op jit(solution)/shard_map/all_to_all | solution.py:191
  213.0 5.6 %all-to-all-done.15 = f32[4,8,1024]{2,1,0:T(8,128)S(1)} async-done(((f32[4,8,1024]{2,1,0:T(8,128)}), f32[4,8,1024]{2,1,0:T(8,128)S(1)}, u32[]{:S(2)}, u32[]{:S(2)}) %all-to-all-start.15) | async-done | bytes 131104 | tf_op jit(solution)/shard_map/all_to_all | solution.py:191
  218.9 0.7 fusion.66
  (175 shorter events, 21.3 us)
Async XLA Ops:
  0.6 63.9 %copy-start = (bf16[1,1024,128]{2,1,0:T(8,128)(2,1)S(1)}, bf16[1,1024,128]{2,1,0:T(8,128)(2,1)}, u32[]{:S(2)}) copy-start(bf16[1,1024,128]{2,1,0:T(8,128)(2,1)} %param.17) | copy-start | bytes 786436
  3.1 21.0 %all-to-all-start.1 = ((bf16[4,8,1]{1,2,0:T(2,128)(2,1)}), bf16[4,8,1]{1,2,0:T(2,128)(2,1)S(1)}, u32[]{:S(2)}, u32[]{:S(2)}) async-start(bf16[4,8,1]{1,2,0:T(2,128)(2,1)} %reshape.598), calls=%async_computation.1 | async-start | bytes 4096 | tf_op jit(solution)/shard_map/all_to_all | solution.py:136
  14.0 2.8 %copy-start.9 = (s32[32]{0:T(128)}, s32[32]{0:T(128)S(1)}, u32[]{:S(2)}) copy-start(s32[32]{0:T(128)S(1)} %multiply_add_fusion.4) | copy-start | bytes 388
  16.8 5.1 %copy-start.6 = (bf16[32,1024]{1,0:T(8,128)(2,1)S(1)}, bf16[32,1024]{1,0:T(8,128)(2,1)}, u32[]{:S(2)}) copy-start(bf16[32,1024]{1,0:T(8,128)(2,1)} %param.15) | copy-start | bytes 196612
  17.5 4.5 %copy-start.11 = (f32[64]{0:T(128)S(1)}, f32[64]{0:T(128)}, u32[]{:S(2)}) copy-start(f32[64]{0:T(128)} %negate_power_fusion) | copy-start | bytes 772
  17.5 4.5 %copy-start.12 = (f32[32]{0:T(128)S(1)}, f32[32]{0:T(128)}, u32[]{:S(2)}) copy-start(f32[32]{0:T(128)} %add_convert_fusion.1) | copy-start | bytes 388
  17.5 5.7 %copy-start.1 = (bf16[32,2,8,1024]{3,2,1,0:T(8,128)(2,1)S(1)}, bf16[32,2,8,1024]{3,2,1,0:T(8,128)(2,1)}, u32[]{:S(2)}) copy-start(bf16[32,2,8,1024]{3,2,1,0:T(8,128)(2,1)} %param.20) | copy-start | bytes 3145732
  21.9 53.4 %copy-start.4 = (bf16[1,2,64,1024]{3,2,1,0:T(8,128)(2,1)S(1)}, bf16[1,2,64,1024]{3,2,1,0:T(8,128)(2,1)}, u32[]{:S(2)}) copy-start(bf16[1,2,64,1024]{3,2,1,0:T(8,128)(2,1)} %param.18) | copy-start | bytes 786436
  23.2 64.0 %copy-start.7 = (bf16[32,1024]{1,0:T(8,128)(2,1)S(1)}, bf16[32,1024]{1,0:T(8,128)(2,1)}, u32[]{:S(2)}) copy-start(bf16[32,1024]{1,0:T(8,128)(2,1)} %param.14) | copy-start | bytes 196612
  24.1 63.4 %copy-start.10 = (s32[32]{0:T(128)S(1)}, s32[32]{0:T(128)}, u32[]{:S(2)}) copy-start(s32[32]{0:T(128)} %copy-done.9) | copy-start | bytes 388
  24.1 69.6 %copy-start.5 = (bf16[32,1,8,128]{3,1,2,0:T(2,128)(2,1)S(1)}, bf16[32,1,8,128]{3,1,2,0:T(2,128)(2,1)}, u32[]{:S(2)}) copy-start(bf16[32,1,8,128]{3,1,2,0:T(2,128)(2,1)} %copy.176) | copy-start | bytes 196612
  24.1 10.8 %all-to-all-start.3 = ((bf16[4,8,4]{1,2,0:T(4,128)(2,1)}), bf16[4,8,4]{1,2,0:T(4,128)(2,1)S(1)}, u32[]{:S(2)}, u32[]{:S(2)}) async-start(bf16[4,8,4]{1,2,0:T(4,128)(2,1)} %copy.178), calls=%async_computation.3 | async-start | bytes 8192 | tf_op jit(solution)/shard_map/all_to_all | solution.py:186
  34.9 8.6 %all-to-all-start.6 = ((bf16[4,8,4]{1,2,0:T(4,128)(2,1)}), bf16[4,8,4]{1,2,0:T(4,128)(2,1)S(1)}, u32[]{:S(2)}, u32[]{:S(2)}) async-start(bf16[4,8,4]{1,2,0:T(4,128)(2,1)} %copy.184), calls=%async_computation.6 | async-start | bytes 8192 | tf_op jit(solution)/shard_map/all_to_all | solution.py:186
  43.5 8.8 %all-to-all-start.9 = ((bf16[4,8,4]{1,2,0:T(4,128)(2,1)}), bf16[4,8,4]{1,2,0:T(4,128)(2,1)S(1)}, u32[]{:S(2)}, u32[]{:S(2)}) async-start(bf16[4,8,4]{1,2,0:T(4,128)(2,1)} %copy.189), calls=%async_computation.9 | async-start | bytes 8192 | tf_op jit(solution)/shard_map/all_to_all | solution.py:186
  52.3 9.0 %all-to-all-start = ((bf16[4,8,1024]{2,1,0:T(8,128)(2,1)}), bf16[4,8,1024]{2,1,0:T(8,128)(2,1)S(1)}, u32[]{:S(2)}, u32[]{:S(2)}) async-start(bf16[4,8,1024]{2,1,0:T(8,128)(2,1)} %fusion.14), calls=%async_computation | async-start | bytes 131072 | tf_op jit(solution)/shard_map/all_to_all | solution.py:135
  61.3 14.9 %all-to-all-start.12 = ((bf16[4,8,4]{1,2,0:T(4,128)(2,1)}), bf16[4,8,4]{1,2,0:T(4,128)(2,1)S(1)}, u32[]{:S(2)}, u32[]{:S(2)}) async-start(bf16[4,8,4]{1,2,0:T(4,128)(2,1)} %copy.194), calls=%async_computation.12 | async-start | bytes 8192 | tf_op jit(solution)/shard_map/all_to_all | solution.py:186
  76.3 10.7 %all-to-all-start.2 = ((bf16[4,8,2048]{2,1,0:T(8,128)(2,1)}), bf16[4,8,2048]{2,1,0:T(8,128)(2,1)S(1)}, u32[]{:S(2)}, u32[]{:S(2)}) async-start(bf16[4,8,2048]{2,1,0:T(8,128)(2,1)} %fusion.52), calls=%async_computation.2 | async-start | bytes 262144 | tf_op jit(solution)/shard_map/all_to_all | solution.py:158
  87.2 7.4 %copy-start.8 = (bf16[32,1024]{1,0:T(8,128)(2,1)S(1)}, bf16[32,1024]{1,0:T(8,128)(2,1)}, u32[]{:S(2)}) copy-start(bf16[32,1024]{1,0:T(8,128)(2,1)} %param.16) | copy-start | bytes 196612
  87.4 8.1 %copy-start.3 = (bf16[32,8,8,128]{3,1,2,0:T(8,128)(2,1)S(1)}, bf16[32,8,8,128]{3,1,2,0:T(8,128)(2,1)}, u32[]{:S(2)}) copy-start(bf16[32,8,8,128]{3,1,2,0:T(8,128)(2,1)} %get-tuple-element.21) | copy-start | bytes 1572868
  90.3 9.0 %all-to-all-start.4 = ((bf16[4,8,1024]{2,1,0:T(8,128)(2,1)}), bf16[4,8,1024]{2,1,0:T(8,128)(2,1)S(1)}, u32[]{:S(2)}, u32[]{:S(2)}) async-start(bf16[4,8,1024]{2,1,0:T(8,128)(2,1)} %fusion.15), calls=%async_computation.4 | async-start | bytes 131072 | tf_op jit(solution)/shard_map/all_to_all | solution.py:185
  95.4 8.2 %copy-start.2 = (bf16[4,1,128,1024]{2,3,0,1:T(8,128)(2,1)S(1)}, bf16[4,1,128,1024]{2,3,0,1:T(8,128)(2,1)}, u32[]{:S(2)}) copy-start(bf16[4,1,128,1024]{2,3,0,1:T(8,128)(2,1)} %copy.259) | copy-start | bytes 3145732
  99.3 9.0 %all-to-all-start.7 = ((bf16[4,8,1024]{2,1,0:T(8,128)(2,1)}), bf16[4,8,1024]{2,1,0:T(8,128)(2,1)S(1)}, u32[]{:S(2)}, u32[]{:S(2)}) async-start(bf16[4,8,1024]{2,1,0:T(8,128)(2,1)} %fusion.16), calls=%async_computation.7 | async-start | bytes 131072 | tf_op jit(solution)/shard_map/all_to_all | solution.py:185
  108.3 9.0 %all-to-all-start.10 = ((bf16[4,8,1024]{2,1,0:T(8,128)(2,1)}), bf16[4,8,1024]{2,1,0:T(8,128)(2,1)S(1)}, u32[]{:S(2)}, u32[]{:S(2)}) async-start(bf16[4,8,1024]{2,1,0:T(8,128)(2,1)} %fusion.17), calls=%async_computation.10 | async-start | bytes 131072 | tf_op jit(solution)/shard_map/all_to_all | solution.py:185
  117.3 9.0 %all-to-all-start.13 = ((bf16[4,8,1024]{2,1,0:T(8,128)(2,1)}), bf16[4,8,1024]{2,1,0:T(8,128)(2,1)S(1)}, u32[]{:S(2)}, u32[]{:S(2)}) async-start(bf16[4,8,1024]{2,1,0:T(8,128)(2,1)} %fusion.18), calls=%async_computation.13 | async-start | bytes 131072 | tf_op jit(solution)/shard_map/all_to_all | solution.py:185
  128.7 12.5 %collective-permute-start = (f32[1,8,8]{1,0,2:T(1,128)S(1)}, f32[1,8,8]{1,0,2:T(1,128)S(1)}, u32[]{:S(2)}, u32[]{:S(2)}) collective-permute-start(f32[1,8,8]{1,0,2:T(1,128)S(1)} %get-tuple-element.31), channel_id=1, source_target_pairs={{0,4},{4,0},{8,12},{12,8},{1,5},{5,1},{9,13},{13,9},{2,6},{6,2},{1... | collective-permute-start | bytes 776 | tf_op jit(solution)/shard_map/ppermute | solution.py:26
  129.7 15.4 %collective-permute-start.1 = (f32[1,8,8]{1,0,2:T(1,128)S(1)}, f32[1,8,8]{1,0,2:T(1,128)S(1)}, u32[]{:S(2)}, u32[]{:S(2)}) collective-permute-start(f32[1,8,8]{1,0,2:T(1,128)S(1)} %get-tuple-element.30), channel_id=1, source_target_pairs={{0,8},{4,12},{8,0},{12,4},{1,9},{5,13},{9,1},{13,5},{2,10},{6,14},... | collective-permute-start | bytes 776 | tf_op jit(solution)/shard_map/ppermute | solution.py:26
  130.1 15.2 %collective-permute-start.2 = (f32[1,8,8]{1,0,2:T(1,128)S(1)}, f32[1,8,8]{1,0,2:T(1,128)S(1)}, u32[]{:S(2)}, u32[]{:S(2)}) collective-permute-start(f32[1,8,8]{1,0,2:T(1,128)S(1)} %get-tuple-element.29), channel_id=1, source_target_pairs={{0,12},{4,8},{8,4},{12,0},{1,13},{5,9},{9,5},{13,1},{2,14},{6,10},... | collective-permute-start | bytes 776 | tf_op jit(solution)/shard_map/ppermute | solution.py:26
  133.2 17.9 %collective-permute-start.3 = (f32[1,8,8]{1,0,2:T(1,128)S(1)}, f32[1,8,8]{1,0,2:T(1,128)S(1)}, u32[]{:S(2)}, u32[]{:S(2)}) collective-permute-start(f32[1,8,8]{1,0,2:T(1,128)S(1)} %get-tuple-element.35), channel_id=1, source_target_pairs={{0,4},{4,0},{8,12},{12,8},{1,5},{5,1},{9,13},{13,9},{2,6},{6,2},{1... | collective-permute-start | bytes 776 | tf_op jit(solution)/shard_map/ppermute | solution.py:26
  133.3 21.7 %collective-permute-start.4 = (f32[1,8,8]{1,0,2:T(1,128)S(1)}, f32[1,8,8]{1,0,2:T(1,128)S(1)}, u32[]{:S(2)}, u32[]{:S(2)}) collective-permute-start(f32[1,8,8]{1,0,2:T(1,128)S(1)} %get-tuple-element.34), channel_id=1, source_target_pairs={{0,8},{4,12},{8,0},{12,4},{1,9},{5,13},{9,1},{13,5},{2,10},{6,14},... | collective-permute-start | bytes 776 | tf_op jit(solution)/shard_map/ppermute | solution.py:26
  134.6 11.5 %all-to-all-start.11 = ((f32[4,8,8]{1,2,0:T(8,128)}), f32[4,8,8]{1,2,0:T(8,128)S(1)}, u32[]{:S(2)}, u32[]{:S(2)}) async-start(f32[4,8,8]{1,2,0:T(8,128)} %copy.192), calls=%async_computation.11 | async-start | bytes 32768 | tf_op jit(solution)/shard_map/all_to_all | solution.py:192
  139.7 78.9 %copy-start.13 = (f32[32,8,1,128]{3,2,1,0:T(1,128)S(1)}, f32[32,8,1,128]{3,2,1,0:T(1,128)}, u32[]{:S(2)}) copy-start(f32[32,8,1,128]{3,2,1,0:T(1,128)} %fusion.28) | copy-start | bytes 393220
  141.2 13.9 %collective-permute-start.5 = (f32[1,8,8]{1,0,2:T(1,128)S(1)}, f32[1,8,8]{1,0,2:T(1,128)S(1)}, u32[]{:S(2)}, u32[]{:S(2)}) collective-permute-start(f32[1,8,8]{1,0,2:T(1,128)S(1)} %get-tuple-element.33), channel_id=1, source_target_pairs={{0,12},{4,8},{8,4},{12,0},{1,13},{5,9},{9,5},{13,1},{2,14},{6,10},... | collective-permute-start | bytes 776 | tf_op jit(solution)/shard_map/ppermute | solution.py:26
  145.2 10.7 %collective-permute-start.6 = (f32[1,8,8]{1,0,2:T(1,128)S(1)}, f32[1,8,8]{1,0,2:T(1,128)S(1)}, u32[]{:S(2)}, u32[]{:S(2)}) collective-permute-start(f32[1,8,8]{1,0,2:T(1,128)S(1)} %get-tuple-element.39), channel_id=1, source_target_pairs={{0,4},{4,0},{8,12},{12,8},{1,5},{5,1},{9,13},{13,9},{2,6},{6,2},{1... | collective-permute-start | bytes 776 | tf_op jit(solution)/shard_map/ppermute | solution.py:26
  145.3 14.4 %collective-permute-start.7 = (f32[1,8,8]{1,0,2:T(1,128)S(1)}, f32[1,8,8]{1,0,2:T(1,128)S(1)}, u32[]{:S(2)}, u32[]{:S(2)}) collective-permute-start(f32[1,8,8]{1,0,2:T(1,128)S(1)} %get-tuple-element.38), channel_id=1, source_target_pairs={{0,8},{4,12},{8,0},{12,4},{1,9},{5,13},{9,1},{13,5},{2,10},{6,14},... | collective-permute-start | bytes 776 | tf_op jit(solution)/shard_map/ppermute | solution.py:26
  146.0 15.5 %all-to-all-start.8 = ((f32[4,8,8]{1,2,0:T(8,128)}), f32[4,8,8]{1,2,0:T(8,128)S(1)}, u32[]{:S(2)}, u32[]{:S(2)}) async-start(f32[4,8,8]{1,2,0:T(8,128)} %copy.187), calls=%async_computation.8 | async-start | bytes 32768 | tf_op jit(solution)/shard_map/all_to_all | solution.py:192
  151.1 8.7 %collective-permute-start.8 = (f32[1,8,8]{1,0,2:T(1,128)S(1)}, f32[1,8,8]{1,0,2:T(1,128)S(1)}, u32[]{:S(2)}, u32[]{:S(2)}) collective-permute-start(f32[1,8,8]{1,0,2:T(1,128)S(1)} %get-tuple-element.37), channel_id=1, source_target_pairs={{0,12},{4,8},{8,4},{12,0},{1,13},{5,9},{9,5},{13,1},{2,14},{6,10},... | collective-permute-start | bytes 776 | tf_op jit(solution)/shard_map/ppermute | solution.py:26
  155.0 4.9 %collective-permute-start.9 = (f32[1,8,8]{1,0,2:T(1,128)S(1)}, f32[1,8,8]{1,0,2:T(1,128)S(1)}, u32[]{:S(2)}, u32[]{:S(2)}) collective-permute-start(f32[1,8,8]{1,0,2:T(1,128)S(1)} %get-tuple-element.43), channel_id=1, source_target_pairs={{0,4},{4,0},{8,12},{12,8},{1,5},{5,1},{9,13},{13,9},{2,6},{6,2},{1... | collective-permute-start | bytes 776 | tf_op jit(solution)/shard_map/ppermute | solution.py:26
  155.1 4.8 %collective-permute-start.10 = (f32[1,8,8]{1,0,2:T(1,128)S(1)}, f32[1,8,8]{1,0,2:T(1,128)S(1)}, u32[]{:S(2)}, u32[]{:S(2)}) collective-permute-start(f32[1,8,8]{1,0,2:T(1,128)S(1)} %get-tuple-element.42), channel_id=1, source_target_pairs={{0,8},{4,12},{8,0},{12,4},{1,9},{5,13},{9,1},{13,5},{2,10},{6,14},... | collective-permute-start | bytes 776 | tf_op jit(solution)/shard_map/ppermute | solution.py:26
  155.9 5.4 %collective-permute-start.11 = (f32[1,8,8]{1,0,2:T(1,128)S(1)}, f32[1,8,8]{1,0,2:T(1,128)S(1)}, u32[]{:S(2)}, u32[]{:S(2)}) collective-permute-start(f32[1,8,8]{1,0,2:T(1,128)S(1)} %get-tuple-element.41), channel_id=1, source_target_pairs={{0,12},{4,8},{8,4},{12,0},{1,13},{5,9},{9,5},{13,1},{2,14},{6,10},... | collective-permute-start | bytes 776 | tf_op jit(solution)/shard_map/ppermute | solution.py:26
  161.5 10.7 %all-to-all-start.14 = ((f32[4,8,8]{1,2,0:T(8,128)}), f32[4,8,8]{1,2,0:T(8,128)S(1)}, u32[]{:S(2)}, u32[]{:S(2)}) async-start(f32[4,8,8]{1,2,0:T(8,128)} %copy.197), calls=%async_computation.14 | async-start | bytes 32768 | tf_op jit(solution)/shard_map/all_to_all | solution.py:192
  172.2 8.8 %all-to-all-start.5 = ((f32[4,8,8]{1,2,0:T(8,128)}), f32[4,8,8]{1,2,0:T(8,128)S(1)}, u32[]{:S(2)}, u32[]{:S(2)}) async-start(f32[4,8,8]{1,2,0:T(8,128)} %copy.182), calls=%async_computation.5 | async-start | bytes 32768 | tf_op jit(solution)/shard_map/all_to_all | solution.py:192
  181.0 9.2 %all-to-all-start.16 = ((f32[4,8,1024]{2,1,0:T(8,128)}), f32[4,8,1024]{2,1,0:T(8,128)S(1)}, u32[]{:S(2)}, u32[]{:S(2)}) async-start(f32[4,8,1024]{2,1,0:T(8,128)} %bitcast.311), calls=%async_computation.16 | async-start | bytes 262144 | tf_op jit(solution)/shard_map/all_to_all | solution.py:191
  190.3 9.8 %all-to-all-start.17 = ((f32[4,8,1024]{2,1,0:T(8,128)}), f32[4,8,1024]{2,1,0:T(8,128)S(1)}, u32[]{:S(2)}, u32[]{:S(2)}) async-start(f32[4,8,1024]{2,1,0:T(8,128)} %bitcast.310), calls=%async_computation.17 | async-start | bytes 262144 | tf_op jit(solution)/shard_map/all_to_all | solution.py:191
  200.1 9.3 %all-to-all-start.18 = ((f32[4,8,1024]{2,1,0:T(8,128)}), f32[4,8,1024]{2,1,0:T(8,128)S(1)}, u32[]{:S(2)}, u32[]{:S(2)}) async-start(f32[4,8,1024]{2,1,0:T(8,128)} %bitcast.309), calls=%async_computation.18 | async-start | bytes 262144 | tf_op jit(solution)/shard_map/all_to_all | solution.py:191
  209.4 9.2 %all-to-all-start.15 = ((f32[4,8,1024]{2,1,0:T(8,128)}), f32[4,8,1024]{2,1,0:T(8,128)S(1)}, u32[]{:S(2)}, u32[]{:S(2)}) async-start(f32[4,8,1024]{2,1,0:T(8,128)} %bitcast.312), calls=%async_computation.15 | async-start | bytes 262144 | tf_op jit(solution)/shard_map/all_to_all | solution.py:191
